TPU v7x, 32 devices: a whole 2x2x4 slice. The times are simulated.
32 devices in a mesh: dp: 8 (over y, x, core), shard: 4 (over z).
Axes of the slice: x: 2, y: 2, z: 4, core: 2. Of those that a mesh axis runs over, the one named last changes fastest.
Arguments:
- grad_parts: bfloat16 [8, 8, 128, 16384], P('dp', None, 'shard'), may hold values from -6 to 6
- first_moment: float32 [1024, 16384], P(('dp', 'shard')), may hold values from -6 to 6
- second_moment: float32 [1024, 16384], P(('dp', 'shard')), may hold values from 0.1 to 16
- master: float32 [1024, 16384], P(('dp', 'shard')), may hold values from -6 to 6
- old_map: int32 [1024], replicated, may hold values from 0 to 1023, as said below
- new_map: int32 [1024], replicated, may hold values from 0 to 1023, as said below
Outputs:
- new_first: float32 [1024, 16384], P(('dp', 'shard'))
- new_second: float32 [1024, 16384], P(('dp', 'shard'))
- new_master: float32 [1024, 16384], P(('dp', 'shard'))
- weights_half: bfloat16 [1024, 16384], P('dp')
Inputs may be any that keep to these rules, and one draw needn't show every extreme that they name: old_map is a permutation of the 1024 block numbers. Row r of either layout belongs to device r // 32. Of the blocks that one device holds in the old layout, exactly one belongs to each device in the new layout. new_map is a permutation of the 1024 block numbers, with the property stated for old_map.
All inputs are finite; a program needn't handle non-finite values.
Results may differ from a plain program's by a relative error of at most 0.0085.
Values may be sent and summed in bfloat16 or wider, within the bound.
No kernel may reach another device: no remote copies, remote signals or barrier semaphores. Data moves between devices by JAX's collectives and lax.ppermute only.
A program may use at most 128 MiB of HBM per device.

v0:
```python
import jax
import jax.numpy as jnp
from jax import lax
from jax.sharding import PartitionSpec as P

beta_one = 0.9
beta_two = 0.95
learning_rate = 0.05
decay_rate = 0.1
epsilon = 1e-08
step_count = 4


def adamw(moment_one, moment_two, weights, gradient):
    new_one = beta_one * moment_one + (1.0 - beta_one) * gradient
    new_two = beta_two * moment_two + (1.0 - beta_two) * gradient * gradient
    unbiased_one = new_one / (1.0 - beta_one**step_count)
    unbiased_two = new_two / (1.0 - beta_two**step_count)
    updated = weights - learning_rate * (
        unbiased_one / (jnp.sqrt(unbiased_two) + epsilon) + decay_rate * weights
    )
    return (new_one, new_two, updated)


def owner_table(blocks, mapping, device_count, span):
    grid = mapping.reshape(device_count, span)
    found = jnp.any(blocks[:, None, None] == grid[None, :, :], axis=2)
    return found.astype(jnp.float32)


def local(grad_parts, first_moment, second_moment, master, old_map, new_map):
    groups = lax.axis_size("dp")
    shard_width = lax.axis_size("shard")
    device_count = groups * shard_width
    my_index = lax.axis_index("dp") * shard_width + lax.axis_index("shard")
    span = first_moment.shape[0]
    block_len = first_moment.shape[1]
    summed_grad = lax.psum_scatter(
        grad_parts[0].astype(jnp.float32).astype(jnp.bfloat16),
        "dp",
        scatter_dimension=0,
        tiled=True,
    ).astype(jnp.float32)[0]
    local_blocks = lax.dynamic_slice_in_dim(old_map, my_index * span, span)
    route = owner_table(local_blocks, new_map, device_count, span)
    packed = jnp.stack([first_moment, second_moment, master], axis=1).reshape(span, 3 * block_len)
    outgoing = jnp.dot(
        route.T, packed, precision=lax.Precision.HIGHEST, preferred_element_type=jnp.float32
    )
    outgoing = outgoing.reshape(device_count, 3, block_len)
    incoming = lax.all_to_all(outgoing, ("dp", "shard"), split_axis=0, concat_axis=0, tiled=True)
    incoming = incoming.reshape(device_count, 3 * block_len)
    wanted = lax.dynamic_slice_in_dim(new_map, my_index * span, span)
    pick = owner_table(wanted, old_map, device_count, span)
    states = jnp.dot(
        pick, incoming, precision=lax.Precision.HIGHEST, preferred_element_type=jnp.float32
    )
    states = states.reshape(span, 3, block_len)
    new_one, new_two, updated = adamw(states[:, 0], states[:, 1], states[:, 2], summed_grad)
    gathered = lax.all_gather(updated.astype(jnp.bfloat16), "shard", axis=0, tiled=True)
    return (new_one, new_two, updated, gathered)


def solution(mesh):
    placed = (
        P("dp", None, "shard", None),
        P(("dp", "shard"), None),
        P(("dp", "shard"), None),
        P(("dp", "shard"), None),
        P(),
        P(),
    )
    return jax.shard_map(
        local,
        mesh=mesh,
        in_specs=placed,
        out_specs=(
            P(("dp", "shard"), None),
            P(("dp", "shard"), None),
            P(("dp", "shard"), None),
            P("dp", None),
        ),
        check_vma=False,
    )
```

profile of v0, /device:TPU:0, one launch (start us, length us, event | category | flops | bytes accessed | tf_op | source)
XLA Modules:
  0.0 326.4 jit_solution(2194416241693857685)
XLA Ops:
  7.2 0.8 eq.35
  7.9 0.8 dynamic_slice.7
  8.7 0.7 compare_reduce_fusion
  9.4 5.3 %fusion.3 = f32[32,3,16384]{2,0,1:T(8,128)S(1)} fusion(pred[32,32]{1,0:T(8,128)(4,1)S(1)} %compare_reduce_fusion, f32[32,1,16384]{2,0,1:T(8,128)} %bitcast.58, f32[32,1,16384]{2,0,1:T(8,128)} %bitcast.59, f32[32,1,16384]{2,0,1:T(8,128)} %bitcast.60), kind=kOutput, calls=%fused_computation.3 | convolution fusion | flops 607125504 | bytes 12583936 | tf_op jit(solution)/shard_map/dot_general | solution.py:47
  14.7 7.5 %copy.21 = f32[32,3,16384]{2,1,0:T(4,128)} copy(f32[32,3,16384]{2,0,1:T(8,128)S(1)} %fusion.3) | data formatting | bytes 12582912 | tf_op jit(solution)/shard_map/dot_general | solution.py:47
  22.3 7.5 %all-to-all-start = ((f32[32,3,16384]{2,1,0:T(4,128)}), f32[32,3,16384]{2,1,0:T(4,128)}, u32[]{:S(2)}, u32[]{:S(2)}) async-start(f32[32,3,16384]{2,1,0:T(4,128)} %copy.21), calls=%async_computation | async-start | bytes 16777216 | tf_op jit(solution)/shard_map/all_to_all | solution.py:51
  29.7 0.0 reduce-scatter.2.cloned.1.call-start
  29.8 0.0 copy-start
  29.8 0.7 reduce-scatter.2.cloned.1.call-update
  30.5 0.2 all-gather.2.cloned.1.call-start
  30.7 0.8 dynamic_slice.6
  31.5 0.0 copy-done
  31.5 0.1 eq.31
  31.5 0.7 compare_reduce_fusion.1
  32.2 178.0 %all-to-all-done = f32[32,3,16384]{2,1,0:T(4,128)} async-done(((f32[32,3,16384]{2,1,0:T(4,128)}), f32[32,3,16384]{2,1,0:T(4,128)}, u32[]{:S(2)}, u32[]{:S(2)}) %all-to-all-start) | async-done | bytes 6291488 | tf_op jit(solution)/shard_map/all_to_all | solution.py:51
  210.2 12.8 %fusion = f32[32,3,16384]{2,0,1:T(8,128)} fusion(pred[32,32]{1,0:T(8,128)(4,1)S(1)} %compare_reduce_fusion.1, f32[4,8,3,16384]{3,2,1,0:T(4,128)} %bitcast.19), kind=kOutput, calls=%fused_computation | convolution fusion | flops 603979776 | bytes 12583936 | tf_op jit(solution)/shard_map/dot_general | solution.py:55
  223.0 0.0 reduce-scatter.2.cloned.1.call-done
  223.0 7.2 %fusion.12 = (bf16[32,16384]{1,0:T(8,128)(2,1)}, f32[32,16384]{1,0:T(8,128)}, f32[32,16384]{1,0:T(8,128)}, f32[32,16384]{1,0:T(8,128)}) fusion(f32[32,3,16384]{2,0,1:T(8,128)} %fusion, bf16[1,32,16384]{2,1,0:T(8,128)(2,1)} %reduce-scatter.2.cloned.1.call-done), kind=kLoop, calls=%fused_computation.22 | loop fusion | flops 8912896 | bytes 14680064 | tf_op jit(solution)/shard_map/convert_element_type | solution.py:60
  230.2 0.0 all-gather.2.cloned.1.call-update
  230.2 84.7 %all-gather.2.cloned.1.call-done = bf16[128,16384]{1,0:T(8,128)(2,1)} async-done(((bf16[32,16384]{1,0:T(8,128)(2,1)}), bf16[128,16384]{1,0:T(8,128)(2,1)}) %all-gather.2.cloned.1.call-update) | async-done | bytes 4194320 | tf_op jit(solution)/shard_map/all_gather | solution.py:60
  315.0 4.6 %copy.44 = bf16[128,16384]{1,0:T(8,128)(2,1)} copy(bf16[128,16384]{1,0:T(8,128)(2,1)} %all-gather.2.cloned.1.call-done) | data formatting | bytes 8388608
Async XLA Ops:
  22.3 187.9 %all-to-all-start = ((f32[32,3,16384]{2,1,0:T(4,128)}), f32[32,3,16384]{2,1,0:T(4,128)}, u32[]{:S(2)}, u32[]{:S(2)}) async-start(f32[32,3,16384]{2,1,0:T(4,128)} %copy.21), calls=%async_computation | async-start | bytes 16777216 | tf_op jit(solution)/shard_map/all_to_all | solution.py:51
  29.7 193.3 %reduce-scatter.2.cloned.1.call-start = ((), (), s32[]{:S(2)}) async-start(), calls=%async_computation.2 | async-start | bytes 9437184 | tf_op jit(solution)/shard_map/reduce_scatter | solution.py:38
  29.8 1.7 copy-start
  30.5 284.5 %all-gather.2.cloned.1.call-start = ((), (), s32[]{:S(2)}) async-start(), calls=%async_computation.3 | async-start | bytes 5242880 | tf_op jit(solution)/shard_map/all_gather | solution.py:60
Sparse Core Ops, SparseCore 0:
  34.0 127.4 reduce-scatter.1
  230.4 84.5 all-gather.1
where the time goes:
time: 327 us; the launch traced here: 326 us
  waiting for transfers between devices  263 us (80%)
  matrix products  18.2 us (6%)
  local copies, waits for them, and re-layouts  14.5 us (4%)
  between operations  14.1 us (4%)
  other arithmetic  8.58 us (3%)
  starting transfers between devices  7.71 us (2%)
    all_to_all x1, waiting for transfers between devices, local(): lax.all_to_all(outgoing, ('dp', 'shard'), split_axis=0, concat_axis=0, ti...  178 us
    all_gather x1, waiting for transfers between devices, local(): lax.all_gather(updated.astype(jnp.bfloat16), 'shard', axis=0, tiled=True)  84.7 us
    dot_general x1, matrix products, local(): jnp.dot(pick, incoming, precision=lax.Precision.HIGHEST, preferred_elemen...  12.8 us
    dot_general x1, local copies, waits for them, and re-layouts, local(): jnp.dot(route.T, packed, precision=lax.Precision.HIGHEST, preferred_eleme...  7.53 us
    all_to_all x1, starting transfers between devices, local(): lax.all_to_all(outgoing, ('dp', 'shard'), split_axis=0, concat_axis=0, ti...  7.45 us
    convert_element_type x1, other arithmetic, local(): updated.astype(jnp.bfloat16)  7.18 us
  transfers between devices with their start and end apart: 3, of which 2 were waited for; matrix products, arithmetic and copies ran while one was open for 4% of the time, Pallas kernels for 0%

commit v1 on v0

v1 whole, which is shorter than its diff:
```python
import jax
import jax.numpy as jnp
from jax import lax
from jax.experimental import pallas as pl
from jax.experimental.pallas import tpu as pltpu
from jax.sharding import PartitionSpec as P


beta_one = 0.9
beta_two = 0.95
learning_rate = 0.05
decay_rate = 0.1
epsilon = 1e-08
step_count = 4
LANES = 128
SUBLANES = 8
CHUNKS = 2
half = jnp.bfloat16
full = jnp.float32
ANY = pl.BlockSpec(memory_space=pl.ANY)
GRANT = pltpu.CompilerParams(vmem_limit_bytes=16 << 20)


def adamw(moment_one, moment_two, weights, gradient):
    new_one = beta_one * moment_one + (1.0 - beta_one) * gradient
    new_two = beta_two * moment_two + (1.0 - beta_two) * gradient * gradient
    unbiased_one = new_one * (1.0 / (1.0 - beta_one**step_count))
    unbiased_two = new_two * (1.0 / (1.0 - beta_two**step_count))
    updated = weights - learning_rate * (
        unbiased_one / (jnp.sqrt(unbiased_two) + epsilon) + decay_rate * weights
    )
    return (new_one, new_two, updated)


def owners(blocks, mapping, span):
    found = blocks[:, :, None] == mapping[:, None, :]
    device = jnp.arange(mapping.shape[1], dtype=jnp.int32) // span
    return jnp.sum(jnp.where(found, device[None, None, :], 0), axis=2)


def in_hbm(array):
    return pltpu.with_memory_space_constraint(array, pltpu.HBM)


def cost(nbytes, flops=0):
    return pl.CostEstimate(flops=flops, bytes_accessed=nbytes, transcendentals=0)


def pack_kernel(dest, *refs):
    arrays, out, rows = refs[:3], refs[-2], refs[-1]
    tiles = arrays[0].shape[1] // LANES
    step = pl.program_id(0)
    for k, array in enumerate(arrays):
        for t in range(tiles):
            rows[k, t * SUBLANES : (t + 1) * SUBLANES] = array[:, t * LANES : (t + 1) * LANES]
    for row in range(SUBLANES):
        to = dest[step * SUBLANES + row]
        for k in range(3):
            line = rows[k, pl.ds(row, tiles, stride=SUBLANES), :]
            out[to, k * tiles : (k + 1) * tiles] = line.astype(half)


def pack(dest, arrays, chunk, width, devices, after):
    span = arrays[0].shape[0]
    tiles = width // LANES
    wide = pl.BlockSpec((SUBLANES, width), lambda i, s: (i, chunk))
    shape = (devices, 3 * tiles, LANES)
    return pl.pallas_call(
        pack_kernel,
        out_shape=jax.ShapeDtypeStruct(shape, half),
        grid_spec=pltpu.PrefetchScalarGridSpec(
            num_scalar_prefetch=1,
            grid=(span // SUBLANES,),
            in_specs=[wide] * 3 + [ANY] * len(after),
            out_specs=pl.BlockSpec(shape, lambda i, s: (0, 0, 0)),
            scratch_shapes=[pltpu.VMEM((3, tiles * SUBLANES, LANES), full)],
        ),
        cost_estimate=cost(18 * span * width),
        compiler_params=GRANT,
    )(dest, *map(in_hbm, arrays), *after)


def send_kernel(bits, grads, *refs):
    refs[-1][...] = grads[...]


def first_send(bits, grads, chunk, width, after):
    groups, span, _ = grads.shape
    return pl.pallas_call(
        send_kernel,
        out_shape=jax.ShapeDtypeStruct((groups // 2, span, width), half),
        grid_spec=pltpu.PrefetchScalarGridSpec(
            num_scalar_prefetch=1,
            grid=(groups // 2,),
            in_specs=[pl.BlockSpec((1, span, width), lambda i, b: (2 * i + 1 - b[0], 0, chunk))] + [ANY] * len(after),
            out_specs=pl.BlockSpec((1, span, width), lambda i, b: (i, 0, 0)),
        ),
        cost_estimate=cost(2 * groups * span * width),
        compiler_params=GRANT,
    )(bits, in_hbm(grads), *after)


def halve_kernel(bits, *refs):
    outs = refs[-4:]
    for k in range(4):
        total = refs[2 * k][...].astype(full) + refs[2 * k + 1][...].astype(full)
        outs[k][...] = total.astype(outs[k].dtype)


def halve(bits, parts, cut, span, after, last):
    specs, operands = [], []
    for kept, kept_at, came, came_col, left, bit in parts:
        place = left[::-1].index(bit)
        for keep in (False, True):

            def combo(i, b, place=place, bit=bit, keep=keep):
                value = b[bit] if keep else 1 - b[bit]
                return ((i >> place) << (place + 1)) | (value << place) | (i & ((1 << place) - 1))

            specs += [
                pl.BlockSpec((1, rows_of(span), cut), lambda i, r, b, combo=combo, at=kept_at: at(combo(i, b), r, b)),
                pl.BlockSpec((1, rows_of(span), cut), lambda i, r, b, combo=combo, col=came_col: (combo(i, b), r, col)),
            ]
            operands += [in_hbm(kept) if kept.ndim == 3 and kept.shape[-1] > cut else kept, came]
    combos = 1 << (len(parts[0][4]) - 1)
    out = pl.BlockSpec((1, rows_of(span), cut), lambda i, r, b: (i, r, 0))
    shape = (combos, span, cut)
    return pl.pallas_call(
        halve_kernel,
        out_shape=[jax.ShapeDtypeStruct(shape, half), jax.ShapeDtypeStruct(shape, full if last else half)] * 2,
        grid_spec=pltpu.PrefetchScalarGridSpec(
            num_scalar_prefetch=1,
            grid=(combos, span // rows_of(span)),
            in_specs=specs + [ANY] * len(after),
            out_specs=[out] * 4,
        ),
        cost_estimate=cost(24 * combos * span * cut),
        compiler_params=GRANT,
    )(bits, *operands, *after)


def rows_of(span):
    return span // 2


def swap(part, bit):
    groups = lax.axis_size("dp")
    return lax.ppermute(part, "dp", [(i, i ^ (1 << bit)) for i in range(groups)])


def update_kernel(source, here, came_in, keep_a, got_a, keep_b, got_b, *refs):
    one_ref, two_ref, master_ref, half_ref, whole_ref, states = refs[-6:]
    tiles = keep_a.shape[2] // LANES
    sub = 2 * tiles
    step = pl.program_id(0)
    for row in range(SUBLANES):
        block = came_in[source[step * SUBLANES + row]].astype(full)
        for k in range(3):
            states[k, pl.ds(row, sub, stride=SUBLANES), :] = block[k * sub : (k + 1) * sub]
    for kept, came, first in ((keep_a, got_a, 0), (keep_b, got_b, tiles)):
        for t in range(tiles):
            cols = slice(t * LANES, (t + 1) * LANES)
            out_cols = slice((first + t) * LANES, (first + t + 1) * LANES)
            rows = slice((first + t) * SUBLANES, (first + t + 1) * SUBLANES)
            gradient = kept[0, :, cols] + came[0, :, cols].astype(full)
            one, two, new = adamw(states[0, rows], states[1, rows], states[2, rows], gradient)
            one_ref[:, out_cols] = one
            two_ref[:, out_cols] = two
            master_ref[:, out_cols] = new
            half_ref[:, out_cols] = new.astype(half)
            whole_ref[:, out_cols] = new.astype(half)


def update(source, here, incoming, terms, carried, chunk, span, block_len, shards, after):
    sub = incoming.shape[1] // 3
    width = sub * LANES
    piece = pl.BlockSpec((1, SUBLANES, width // 2), lambda i, s, h: (0, i, 0))
    wide = pl.BlockSpec((SUBLANES, width), lambda i, s, h: (i, chunk))
    tile_rows = span // SUBLANES
    whole = pl.BlockSpec((SUBLANES, width), lambda i, s, h: (h[0] * tile_rows + i, chunk))
    outs = [jax.ShapeDtypeStruct((span, block_len), full)] * 3 + [
        jax.ShapeDtypeStruct((span, width), half),
        jax.ShapeDtypeStruct((shards * span, block_len), half),
    ]
    spread = {7 + i: o for i, o in enumerate((0, 1, 2, 4))} if carried else {}
    return pl.pallas_call(
        update_kernel,
        out_shape=outs,
        grid_spec=pltpu.PrefetchScalarGridSpec(
            num_scalar_prefetch=2,
            grid=(tile_rows,),
            in_specs=[pl.BlockSpec(incoming.shape, lambda i, s, h: (0, 0, 0))]
            + [piece] * 4
            + [ANY] * (len(carried) + len(after)),
            out_specs=[wide] * 3 + [pl.BlockSpec((SUBLANES, width), lambda i, s, h: (i, 0)), whole],
            scratch_shapes=[pltpu.VMEM((3, sub * SUBLANES, LANES), full)],
        ),
        input_output_aliases=spread,
        cost_estimate=cost(26 * span * width, 20 * span * width),
        compiler_params=GRANT,
    )(source, here, in_hbm(incoming), *map(in_hbm, terms), *carried, *after)


def exchange(outgoing):
    return lax.all_to_all(outgoing, ("dp", "shard"), split_axis=0, concat_axis=0, tiled=True)


def gather_steps(block, last):
    n = lax.axis_size("shard")
    up, down = {0: block}, {0: block}
    if last and n == 4:
        near = lax.ppermute(block, "shard", [(i, (i + 1) % n) for i in range(n)])
        back = lax.ppermute(block, "shard", [((i + 1) % n, i) for i in range(n)])
        over = lax.ppermute(near, "shard", [(i, i + 1) for i in range(1, n - 1)])
        under = lax.ppermute(back, "shard", [(i + 1, i) for i in range(n - 2)])
        return {1: (near, near), 3: (back, back), 2: (over, under)}
    for step in range(1, n):
        up[step] = lax.ppermute(up[step - 1], "shard", [(i, i + 1) for i in range(step - 1, n - 1)])
        down[step] = lax.ppermute(down[step - 1], "shard", [(i + 1, i) for i in range(n - step)])
    return {far: (up[far], down[n - far]) for far in range(1, n)}


def place(whole, came, column):
    n = lax.axis_size("shard")
    here = lax.axis_index("shard")
    for far, (below, above) in came.items():
        value = below if below is above else jnp.where(here >= far, below, above)
        whole = lax.dynamic_update_slice(whole, value, ((here + n - far) % n * value.shape[0], column))
    return whole


def local(grad_parts, first_moment, second_moment, master, old_map, new_map):
    groups = lax.axis_size("dp")
    shards = lax.axis_size("shard")
    devices = groups * shards
    here = lax.axis_index("shard")
    replica = lax.axis_index("dp")
    mine = replica * shards + here
    span, block_len = first_moment.shape
    chunks = CHUNKS if block_len % (CHUNKS * 2 * SUBLANES * LANES) == 0 else 1
    width = block_len // chunks
    cut = width // 2
    grads = grad_parts[0]
    maps = jnp.stack([old_map, new_map])
    dest, source = owners(lax.dynamic_slice_in_dim(maps, mine * span, span, 1), maps[::-1], span)
    at = here.reshape(1).astype(jnp.int32)
    steps = groups.bit_length() - 1
    bits = ((replica >> jnp.arange(steps, dtype=jnp.int32)) & 1).astype(jnp.int32)
    left = list(range(steps))[::-1][:-1]
    orders = (left[::-1], left)
    states = (first_moment, second_moment, master)

    def first_parts(c, came):
        return [
            (grads, lambda j, r, b, h=h: (2 * j + b[0], r, 2 * c + h), came, h, left, orders[h][0]) for h in range(2)
        ]

    def next_parts(c, s, came):
        return [
            (sums[c][2 * h + 1], lambda j, r, b: (j, r, 0), came[h], 0, [b for b in left if b not in orders[h][:s]], orders[h][s])
            for h in range(2)
        ]

    def swaps(c, s):
        return [swap(sums[c][2 * h], orders[h][s]) for h in range(2)]

    def finish_sum(c, after):
        for s in range(1, len(left)):
            came = swaps(c, s - 1)
            sums[c] = halve(bits, next_parts(c, s, came), cut, span, after, s == len(left) - 1)
            after = [sums[c][0]]
        return after

    outgoing, incoming, pair, sums, carried = {}, {}, {}, {}, []
    last = chunks - 1
    short = len(left) == 1
    outgoing[0] = pack(dest, states, 0, width, devices, [])
    incoming[0] = exchange(outgoing[0])
    after = [outgoing[0]]
    for c in range(chunks):
        sent = first_send(bits, grads, c, width, after)
        after = [sent]
        pair[c] = swap(sent, 0)
    sums[0] = halve(bits, first_parts(0, pair[0]), cut, span, after, short)
    after = [sums[0][0]]
    for c in range(1, chunks):
        outgoing[c] = pack(dest, states, c, width, devices, after)
        after = [outgoing[c]]
        sums[c] = halve(bits, first_parts(c, pair[c]), cut, span, after, short)
        after = [sums[c][0]]
    after = finish_sum(0, after)
    gathered = []
    for c in range(chunks):
        if c < last:
            incoming[c + 1] = exchange(outgoing[c + 1])
        came = swaps(c, len(left) - 1)
        terms = [sums[c][1], came[0], sums[c][3], came[1]]
        one, two, new, block, whole = update(source, at, incoming[c], terms, carried, c, span, block_len, shards, after)
        carried = [one, two, new, whole]
        after = [block]
        gathered.append(gather_steps(block, c == last))
        if c < last:
            after = finish_sum(c + 1, after) + [gathered[c][1][0]]
    for c in range(chunks):
        whole = place(whole, gathered[c], c * width)
    return (one, two, new, whole)


def solution(mesh):
    placed = (
        P("dp", None, "shard", None),
        P(("dp", "shard"), None),
        P(("dp", "shard"), None),
        P(("dp", "shard"), None),
        P(),
        P(),
    )
    return jax.shard_map(
        local,
        mesh=mesh,
        in_specs=placed,
        out_specs=(
            P(("dp", "shard"), None),
            P(("dp", "shard"), None),
            P(("dp", "shard"), None),
            P("dp", None),
        ),
        check_vma=False,
    )
```

time: 327 us -> 191 us (0.58)
  waiting for transfers between devices: 263 us -> 99.6 us
  Pallas kernels: 0 us -> 35.5 us
  starting transfers between devices: 7.71 us -> 38.4 us
  matrix products: 18.2 us -> 0 us
  between operations: 14.1 us -> 0.87 us
  local copies, waits for them, and re-layouts: 14.5 us -> 9.89 us
    all_to_all x1 -> x2, waiting for transfers between devices: 178 us -> 18.3 us  [exchange(): lax.all_to_all(outgoing, ('dp', 'shard'), split_axis=0, concat_axis=0, ti...]
    all_gather x1 -> x0, waiting for transfers between devices: 84.7 us -> none  [local(): lax.all_gather(updated.astype(jnp.bfloat16), 'shard', axis=0, tiled=True)]
    ppermute x0 -> x20, waiting for transfers between devices: none -> 81.4 us  [the longest x10 33 us: swap(): return lax.ppermute(part, 'dp', [(i, i ^ 1 << bit) for i in range(groups)])]
    pallas_call x0 -> x10, Pallas kernels: none -> 35.5 us  [the longest x2 11.6 us: update(): pl.pallas_call(update_kernel, out_shape=outs, grid_spec=pltpu.PrefetchSca...]
    ppermute x0 -> x20, starting transfers between devices: none -> 26.1 us  [the longest x10 9.74 us: swap(): return lax.ppermute(part, 'dp', [(i, i ^ 1 << bit) for i in range(groups)])]
    dot_general x2 -> x0, matrix products: 18.2 us -> none  [the longest x1 12.8 us: local(): jnp.dot(pick, incoming, precision=lax.Precision.HIGHEST, preferred_elemen...]
    dot_general x1 -> x0, local copies, waits for them, and re-layouts: 7.53 us -> none  [local(): jnp.dot(route.T, packed, precision=lax.Precision.HIGHEST, preferred_eleme...]
    convert_element_type x1 -> x0, other arithmetic: 7.18 us -> none  [local(): updated.astype(jnp.bfloat16)]
  transfers between devices with their start and end apart: 3 -> 22, of which waited for: 2 -> 12; matrix products, arithmetic and copies ran while one was open for 4% -> 2% of each run, Pallas kernels for 0% -> 16%
where the time goes in v1:
time: 191 us; the launch traced here: 190 us
  waiting for transfers between devices  99.6 us (52%)
  starting transfers between devices  38.4 us (20%)
  Pallas kernels  35.5 us (19%)
  local copies, waits for them, and re-layouts  9.89 us (5%)
  other arithmetic  5.36 us (3%)
    ppermute x10, waiting for transfers between devices, swap(): return lax.ppermute(part, 'dp', [(i, i ^ 1 << bit) for i in range(groups)])  33 us
    ppermute x3, waiting for transfers between devices, gather_steps(): lax.ppermute(down[step - 1], 'shard', [(i + 1, i) for i in range(n - step)])  19 us
    all_to_all x2, waiting for transfers between devices, exchange(): lax.all_to_all(outgoing, ('dp', 'shard'), split_axis=0, concat_axis=0, ti...  18.3 us
    ppermute x1, waiting for transfers between devices, gather_steps(): under = lax.ppermute(back, 'shard', [(i + 1, i) for i in range(n - 2)])  13.6 us
    all_to_all x2, starting transfers between devices, exchange(): lax.all_to_all(outgoing, ('dp', 'shard'), split_axis=0, concat_axis=0, ti...  12.3 us
    pallas_call x2, Pallas kernels, update(): pl.pallas_call(update_kernel, out_shape=outs, grid_spec=pltpu.PrefetchSca...  11.6 us
    ppermute x1, waiting for transfers between devices, gather_steps(): near = lax.ppermute(block, 'shard', [(i, (i + 1) % n) for i in range(n)])  9.99 us
    ppermute x10, starting transfers between devices, swap(): return lax.ppermute(part, 'dp', [(i, i ^ 1 << bit) for i in range(groups)])  9.74 us
  transfers between devices with their start and end apart: 22, of which 12 were waited for; matrix products, arithmetic and copies ran while one was open for 2% of the time, Pallas kernels for 16%

profile of v1, /device:TPU:0, one launch (start us, length us, event | category | flops | bytes accessed | tf_op | source)
XLA Modules:
  0.0 189.6 jit_solution(15857554311513536079)
XLA Ops:
  0.7 0.7 pad_add_fusion
  1.4 0.8 fusion.3
  2.1 0.2 rev.3
  2.3 0.2 select_reduce_fusion
  2.5 4.6 %shard_map.93.refs_0_ = bf16[32,192,128]{2,1,0:T(8,128)(2,1)} custom-call(s32[32]{0:T(128)S(1)} %get-tuple-element.56.dest, f32[32,16384]{1,0:T(8,128)} %refs_0_.3, f32[32,16384]{1,0:T(8,128)} %refs_1_.3, f32[32,16384]{1,0:T(8,128)} %refs_2_.3), custom_call_target="tpu_custom_call" | custom-call | bytes 4718592 | tf_op jit(solution)/shard_map/pallas_call | solution.py:68
  7.1 7.4 %all-to-all-start.1 = ((bf16[32,192,128]{2,1,0:T(8,128)(2,1)}), bf16[32,192,128]{2,1,0:T(8,128)(2,1)}, u32[]{:S(2)}, u32[]{:S(2)}) async-start(bf16[32,192,128]{2,1,0:T(8,128)(2,1)} %shard_map.93.refs_0_), calls=%async_computation.1 | async-start | bytes 3145728 | tf_op jit(solution)/shard_map/all_to_all | solution.py:205
  14.6 2.9 %shard_map.94.refs_0_ = bf16[4,32,8192]{2,1,0:T(8,128)(2,1)S(1)} custom-call(s32[3]{0:T(128)S(1)} %shift-right-arithmetic_and_fusion.bits, bf16[8,32,16384]{2,1,0:T(8,128)(2,1)} %bitcast.8, bf16[32,192,128]{2,1,0:T(8,128)(2,1)} %shard_map.93.refs_0_), custom_call_target="tpu_custom_call" | custom-call | bytes 4194304 | tf_op jit(solution)/shard_map/pallas_call | solution.py:89
  17.5 0.3 collective-permute-start
  17.8 4.3 %shard_map.95.refs_8_ = bf16[4,32,8192]{2,1,0:T(8,128)(2,1)} custom-call(s32[3]{0:T(128)S(1)} %shift-right-arithmetic_and_fusion.bits, bf16[8,32,16384]{2,1,0:T(8,128)(2,1)} %bitcast.9, bf16[4,32,8192]{2,1,0:T(8,128)(2,1)S(1)} %shard_map.94.refs_0_), custom_call_target="tpu_custom_call" | custom-call | bytes 4194304 | tf_op jit(solution)/shard_map/pallas_call | solution.py:89
  22.1 0.3 collective-permute-start.1
  22.4 3.5 %shard_map.96 = (bf16[2,32,4096]{2,1,0:T(8,128)(2,1)S(1)}, bf16[2,32,4096]{2,1,0:T(8,128)(2,1)S(1)}, bf16[2,32,4096]{2,1,0:T(8,128)(2,1)S(1)}, bf16[2,32,4096]{2,1,0:T(8,128)(2,1)S(1)}) custom-call(s32[3]{0:T(128)S(1)} %shift-right-arithmetic_and_fusion.bits, bf16[8,32,16384]{2,1,0:T(8,128)(2,1)} %bitcast.10, ...), custom_call_target="tpu_custom_call" | custom-call | bytes 6291456 | tf_op jit(solution)/shard_map/pallas_call | solution.py:128
  25.9 0.8 copy-done.7
  26.7 3.4 %shard_map.97.refs_8_ = bf16[32,192,128]{2,1,0:T(8,128)(2,1)S(1)} custom-call(s32[32]{0:T(128)S(1)} %get-tuple-element.56.dest, f32[32,16384]{1,0:T(8,128)} %refs_0_.3, f32[32,16384]{1,0:T(8,128)} %refs_1_.3, f32[32,16384]{1,0:T(8,128)} %refs_2_.3, bf16[2,32,4096]{2,1,0:T(8,128)(2,1)S(1)} %get-tuple-element.30.refs_3_), custom_call_target="tpu_custom_call" | custom-call | bytes 4718592 | tf_op jit(solution)/shard_map/pallas_call | solution.py:68
  30.2 1.1 copy-done
  31.3 0.8 copy-done.4
  32.1 18.3 %all-to-all-done.1.came_in = bf16[32,192,128]{2,1,0:T(8,128)(2,1)} async-done(((bf16[32,192,128]{2,1,0:T(8,128)(2,1)}), bf16[32,192,128]{2,1,0:T(8,128)(2,1)}, u32[]{:S(2)}, u32[]{:S(2)}) %all-to-all-start.1) | async-done | bytes 1572896 | tf_op jit(solution)/shard_map/all_to_all | solution.py:205
  50.4 4.8 %all-to-all-start = ((bf16[32,192,128]{2,1,0:T(8,128)(2,1)}), bf16[32,192,128]{2,1,0:T(8,128)(2,1)}, u32[]{:S(2)}, u32[]{:S(2)}) async-start(bf16[32,192,128]{2,1,0:T(8,128)(2,1)} %copy-done), calls=%async_computation | async-start | bytes 3145728 | tf_op jit(solution)/shard_map/all_to_all | solution.py:205
  55.2 1.8 collective-permute-start.4
  57.0 1.5 collective-permute-start.5
  58.4 1.4 copy-done.1
  59.9 3.5 %shard_map.98 = (bf16[2,32,4096]{2,1,0:T(8,128)(2,1)S(1)}, bf16[2,32,4096]{2,1,0:T(8,128)(2,1)S(1)}, bf16[2,32,4096]{2,1,0:T(8,128)(2,1)S(1)}, bf16[2,32,4096]{2,1,0:T(8,128)(2,1)S(1)}) custom-call(s32[3]{0:T(128)S(1)} %shift-right-arithmetic_and_fusion.bits, bf16[8,32,16384]{2,1,0:T(8,128)(2,1)} %bitcast.14, ...), custom_call_target="tpu_custom_call" | custom-call | bytes 6291456 | tf_op jit(solution)/shard_map/pallas_call | solution.py:128
  63.3 19.8 %collective-permute-done.4.refs_1_.refs_3_ = bf16[2,32,4096]{2,1,0:T(8,128)(2,1)S(1)} collective-permute-done((bf16[2,32,4096]{2,1,0:T(8,128)(2,1)}, bf16[2,32,4096]{2,1,0:T(8,128)(2,1)S(1)}, u32[]{:S(2)}, u32[]{:S(2)}) %collective-permute-start.4) | collective-permute-done | bytes 524320 | tf_op jit(solution)/shard_map/ppermute | solution.py:148
  83.1 1.1 collective-permute-done.5.refs_5_.refs_7_
  84.2 0.8 shard_map.99
  85.0 0.8 copy-done.5
  85.8 0.8 copy-done.6
  86.6 0.4 collective-permute-start.6
  87.0 0.6 collective-permute-start.7
  87.6 7.8 %collective-permute-done.6.got_a = bf16[1,32,4096]{2,1,0:T(8,128)(2,1)S(1)} collective-permute-done((bf16[1,32,4096]{2,1,0:T(8,128)(2,1)S(1)}, bf16[1,32,4096]{2,1,0:T(8,128)(2,1)S(1)}, u32[]{:S(2)}, u32[]{:S(2)}) %collective-permute-start.6) | collective-permute-done | bytes 262176 | tf_op jit(solution)/shard_map/ppermute | solution.py:148
  95.4 0.1 collective-permute-done.7.got_b
  95.5 0.6 copy-done.9
  96.1 0.1 copy-done.10
  96.2 5.8 %shard_map.100 = (f32[32,16384]{1,0:T(8,128)}, f32[32,16384]{1,0:T(8,128)}, f32[32,16384]{1,0:T(8,128)}, bf16[32,8192]{1,0:T(8,128)(2,1)S(1)}, bf16[128,16384]{1,0:T(8,128)(2,1)}) custom-call(s32[32]{0:T(128)S(1)} %get-tuple-element.57.source, s32[1]{0:T(128)} %bitcast.3.here, bf16[32,192,128]{2,1,0:T(8,128)(2,1)} %all-to-all-done.1.came_in, ...), custom_call_target="tpu_custom_call" | custom-call | flops 5242880 | bytes 6815744 | tf_op jit(solution)/shard_map/pallas_call | solution.py:186
  102.0 1.3 collective-permute-start.11
  103.3 4.6 %collective-permute-start.10 = (bf16[32,8192]{1,0:T(8,128)(2,1)S(1)}, bf16[32,8192]{1,0:T(8,128)(2,1)S(1)}, u32[]{:S(2)}, u32[]{:S(2)}) collective-permute-start(bf16[32,8192]{1,0:T(8,128)(2,1)S(1)} %get-tuple-element.42.refs_8_), channel_id=1, source_target_pairs={{0,1},{1,2},{2,3},{4,5},{5,6},{6,7},{8,9},{9,10},{10,11},{12,13},{... | collective-permute-start | bytes 1572872 | tf_op jit(solution)/shard_map/ppermute | solution.py:218
  107.9 9.2 %collective-permute-done.11 = bf16[32,8192]{1,0:T(8,128)(2,1)S(1)} collective-permute-done((bf16[32,8192]{1,0:T(8,128)(2,1)S(1)}, bf16[32,8192]{1,0:T(8,128)(2,1)S(1)}, u32[]{:S(2)}, u32[]{:S(2)}) %collective-permute-start.11) | collective-permute-done | bytes 524320 | tf_op jit(solution)/shard_map/ppermute | solution.py:219
  117.1 1.3 collective-permute-start.12
  118.4 1.0 collective-permute-start.2
  119.3 1.5 collective-permute-start.3
  120.9 0.7 collective-permute-start.14
  121.5 9.8 %collective-permute-done.12 = bf16[32,8192]{1,0:T(8,128)(2,1)S(1)} collective-permute-done((bf16[32,8192]{1,0:T(8,128)(2,1)S(1)}, bf16[32,8192]{1,0:T(8,128)(2,1)S(1)}, u32[]{:S(2)}, u32[]{:S(2)}) %collective-permute-start.12) | collective-permute-done | bytes 524320 | tf_op jit(solution)/shard_map/ppermute | solution.py:219
  131.3 1.3 collective-permute-start.13
  132.6 0.8 shard_map.101
  133.5 0.8 copy-done.2
  134.2 0.8 copy-done.3
  135.0 1.7 collective-permute-start.8
  136.7 0.8 collective-permute-start.9
  137.5 1.4 collective-permute-start.15
  139.0 2.5 %collective-permute-done.8.got_a = bf16[1,32,4096]{2,1,0:T(8,128)(2,1)S(1)} collective-permute-done((bf16[1,32,4096]{2,1,0:T(8,128)(2,1)S(1)}, bf16[1,32,4096]{2,1,0:T(8,128)(2,1)S(1)}, u32[]{:S(2)}, u32[]{:S(2)}) %collective-permute-start.8) | collective-permute-done | bytes 262176 | tf_op jit(solution)/shard_map/ppermute | solution.py:148
  141.5 1.7 collective-permute-done.9.got_b
  143.2 5.8 %shard_map.102 = (f32[32,16384]{1,0:T(8,128)}, f32[32,16384]{1,0:T(8,128)}, f32[32,16384]{1,0:T(8,128)}, bf16[32,8192]{1,0:T(8,128)(2,1)S(1)}, bf16[128,16384]{1,0:T(8,128)(2,1)}) custom-call(s32[32]{0:T(128)S(1)} %get-tuple-element.57.source, s32[1]{0:T(128)} %bitcast.3.here, ...), custom_call_target="tpu_custom_call", output_to_operand_aliasing={{0}: (7, {}), {1}: (8, {}), {2}: (9, {}), {4}: (10, {})} | custom-call | flops 5242880 | bytes 6815744 | tf_op jit(solution)/shard_map/pallas_call | solution.py:186
  149.0 2.7 %collective-permute-start.16 = (bf16[32,8192]{1,0:T(8,128)(2,1)S(1)}, bf16[32,8192]{1,0:T(8,128)(2,1)S(1)}, u32[]{:S(2)}, u32[]{:S(2)}) collective-permute-start(bf16[32,8192]{1,0:T(8,128)(2,1)S(1)} %get-tuple-element.55), channel_id=1, source_target_pairs={{0,1},{1,2},{2,3},{3,0},{4,5},{5,6},{6,7},{7,4},{8,9},{9,10},{10,1... | collective-permute-start | bytes 1572872 | tf_op jit(solution)/shard_map/ppermute | solution.py:212
  151.7 1.2 collective-permute-start.17
  152.8 0.9 select_dynamic-update-slice_fusion.3
  153.8 0.9 select_dynamic-update-slice_fusion.2
  154.7 0.9 select_dynamic-update-slice_fusion.1
  155.6 10.0 %collective-permute-done.16 = bf16[32,8192]{1,0:T(8,128)(2,1)S(1)} collective-permute-done((bf16[32,8192]{1,0:T(8,128)(2,1)S(1)}, bf16[32,8192]{1,0:T(8,128)(2,1)S(1)}, u32[]{:S(2)}, u32[]{:S(2)}) %collective-permute-start.16) | collective-permute-done | bytes 524320 | tf_op jit(solution)/shard_map/ppermute | solution.py:212
  165.6 0.7 collective-permute-start.18
  166.3 0.8 constant_dynamic-update-slice_fusion.1
  167.1 5.8 %collective-permute-done.17 = bf16[32,8192]{1,0:T(8,128)(2,1)S(1)} collective-permute-done((bf16[32,8192]{1,0:T(8,128)(2,1)S(1)}, bf16[32,8192]{1,0:T(8,128)(2,1)S(1)}, u32[]{:S(2)}, u32[]{:S(2)}) %collective-permute-start.17) | collective-permute-done | bytes 524320 | tf_op jit(solution)/shard_map/ppermute | solution.py:213
  172.9 1.3 collective-permute-start.19
  174.2 0.8 constant_dynamic-update-slice_fusion
  175.1 13.6 %collective-permute-done.19 = bf16[32,8192]{1,0:T(8,128)(2,1)S(1)} collective-permute-done((bf16[32,8192]{1,0:T(8,128)(2,1)S(1)}, bf16[32,8192]{1,0:T(8,128)(2,1)S(1)}, u32[]{:S(2)}, u32[]{:S(2)}) %collective-permute-start.19) | collective-permute-done | bytes 524320 | tf_op jit(solution)/shard_map/ppermute | solution.py:215
  188.7 0.9 select_dynamic-update-slice_fusion
  (25 shorter events, 0.1 us)
Async XLA Ops:
  7.1 43.2 %all-to-all-start.1 = ((bf16[32,192,128]{2,1,0:T(8,128)(2,1)}), bf16[32,192,128]{2,1,0:T(8,128)(2,1)}, u32[]{:S(2)}, u32[]{:S(2)}) async-start(bf16[32,192,128]{2,1,0:T(8,128)(2,1)} %shard_map.93.refs_0_), calls=%async_computation.1 | async-start | bytes 3145728 | tf_op jit(solution)/shard_map/all_to_all | solution.py:205
  17.5 4.9 %collective-permute-start = (bf16[4,32,8192]{2,1,0:T(8,128)(2,1)S(1)}, bf16[4,32,8192]{2,1,0:T(8,128)(2,1)S(1)}, u32[]{:S(2)}, u32[]{:S(2)}) collective-permute-start(bf16[4,32,8192]{2,1,0:T(8,128)(2,1)S(1)} %shard_map.94.refs_0_), channel_id=1, source_target_pairs={{0,4},{4,0},{8,12},{12,8},{16,20},{20,16},{24,28},{28,24},{1,5},{5... | collective-permute-start | bytes 6291464 | tf_op jit(solution)/shard_map/ppermute | solution.py:148
  22.1 36.4 %collective-permute-start.1 = (bf16[4,32,8192]{2,1,0:T(8,128)(2,1)}, bf16[4,32,8192]{2,1,0:T(8,128)(2,1)S(1)}, u32[]{:S(2)}, u32[]{:S(2)}) collective-permute-start(bf16[4,32,8192]{2,1,0:T(8,128)(2,1)} %shard_map.95.refs_8_), channel_id=1, source_target_pairs={{0,4},{4,0},{8,12},{12,8},{16,20},{20,16},{24,28},{28,24},{1,5},{5... | collective-permute-start | bytes 6291464 | tf_op jit(solution)/shard_map/ppermute | solution.py:148
  25.9 0.8 copy-start.7
  30.1 1.1 copy-start
  31.3 0.8 copy-start.4
  50.4 92.8 %all-to-all-start = ((bf16[32,192,128]{2,1,0:T(8,128)(2,1)}), bf16[32,192,128]{2,1,0:T(8,128)(2,1)}, u32[]{:S(2)}, u32[]{:S(2)}) async-start(bf16[32,192,128]{2,1,0:T(8,128)(2,1)} %copy-done), calls=%async_computation | async-start | bytes 3145728 | tf_op jit(solution)/shard_map/all_to_all | solution.py:205
  55.2 27.9 %collective-permute-start.4 = (bf16[2,32,4096]{2,1,0:T(8,128)(2,1)}, bf16[2,32,4096]{2,1,0:T(8,128)(2,1)S(1)}, u32[]{:S(2)}, u32[]{:S(2)}) collective-permute-start(bf16[2,32,4096]{2,1,0:T(8,128)(2,1)} %copy-done.4), channel_id=1, source_target_pairs={{0,8},{4,12},{8,0},{12,4},{16,24},{20,28},{24,16},{28,20},{1,9},{5... | collective-permute-start | bytes 1572872 | tf_op jit(solution)/shard_map/ppermute | solution.py:148
  57.0 27.2 %collective-permute-start.5 = (bf16[2,32,4096]{2,1,0:T(8,128)(2,1)}, bf16[2,32,4096]{2,1,0:T(8,128)(2,1)S(1)}, u32[]{:S(2)}, u32[]{:S(2)}) collective-permute-start(bf16[2,32,4096]{2,1,0:T(8,128)(2,1)} %copy-done.7), channel_id=1, source_target_pairs={{0,16},{4,20},{8,24},{12,28},{16,0},{20,4},{24,8},{28,12},{1,17},{... | collective-permute-start | bytes 1572872 | tf_op jit(solution)/shard_map/ppermute | solution.py:148
  58.4 1.4 copy-start.1
  85.0 0.8 copy-start.5
  85.8 0.8 copy-start.6
  86.6 8.8 %collective-permute-start.6 = (bf16[1,32,4096]{2,1,0:T(8,128)(2,1)S(1)}, bf16[1,32,4096]{2,1,0:T(8,128)(2,1)S(1)}, u32[]{:S(2)}, u32[]{:S(2)}) collective-permute-start(bf16[1,32,4096]{2,1,0:T(8,128)(2,1)S(1)} %get-tuple-element.39.refs_0_), channel_id=1, source_target_pairs={{0,16},{4,20},{8,24},{12,28},{16,0},{20,4},{24,8},{28,12},{1,17},{... | collective-permute-start | bytes 786440 | tf_op jit(solution)/shard_map/ppermute | solution.py:148
  87.0 8.5 %collective-permute-start.7 = (bf16[1,32,4096]{2,1,0:T(8,128)(2,1)S(1)}, bf16[1,32,4096]{2,1,0:T(8,128)(2,1)S(1)}, u32[]{:S(2)}, u32[]{:S(2)}) collective-permute-start(bf16[1,32,4096]{2,1,0:T(8,128)(2,1)S(1)} %get-tuple-element.41), channel_id=1, source_target_pairs={{0,8},{4,12},{8,0},{12,4},{16,24},{20,28},{24,16},{28,20},{1,9},{5... | collective-permute-start | bytes 786440 | tf_op jit(solution)/shard_map/ppermute | solution.py:148
  95.4 0.7 copy-start.9
  95.5 0.7 copy-start.10
  102.0 15.1 %collective-permute-start.11 = (bf16[32,8192]{1,0:T(8,128)(2,1)S(1)}, bf16[32,8192]{1,0:T(8,128)(2,1)S(1)}, u32[]{:S(2)}, u32[]{:S(2)}) collective-permute-start(bf16[32,8192]{1,0:T(8,128)(2,1)S(1)} %get-tuple-element.42.refs_8_), channel_id=1, source_target_pairs={{1,0},{2,1},{3,2},{5,4},{6,5},{7,6},{9,8},{10,9},{11,10},{13,12},{... | collective-permute-start | bytes 1572872 | tf_op jit(solution)/shard_map/ppermute | solution.py:219
  103.3 17.5 %collective-permute-start.10 = (bf16[32,8192]{1,0:T(8,128)(2,1)S(1)}, bf16[32,8192]{1,0:T(8,128)(2,1)S(1)}, u32[]{:S(2)}, u32[]{:S(2)}) collective-permute-start(bf16[32,8192]{1,0:T(8,128)(2,1)S(1)} %get-tuple-element.42.refs_8_), channel_id=1, source_target_pairs={{0,1},{1,2},{2,3},{4,5},{5,6},{6,7},{8,9},{9,10},{10,11},{12,13},{... | collective-permute-start | bytes 1572872 | tf_op jit(solution)/shard_map/ppermute | solution.py:218
  117.1 14.2 %collective-permute-start.12 = (bf16[32,8192]{1,0:T(8,128)(2,1)S(1)}, bf16[32,8192]{1,0:T(8,128)(2,1)S(1)}, u32[]{:S(2)}, u32[]{:S(2)}) collective-permute-start(bf16[32,8192]{1,0:T(8,128)(2,1)S(1)} %collective-permute-done.11), channel_id=1, source_target_pairs={{1,0},{2,1},{5,4},{6,5},{9,8},{10,9},{13,12},{14,13},{17,16},{18,1... | collective-permute-start | bytes 1572872 | tf_op jit(solution)/shard_map/ppermute | solution.py:219
  118.4 14.2 %collective-permute-start.2 = (bf16[2,32,4096]{2,1,0:T(8,128)(2,1)S(1)}, bf16[2,32,4096]{2,1,0:T(8,128)(2,1)S(1)}, u32[]{:S(2)}, u32[]{:S(2)}) collective-permute-start(bf16[2,32,4096]{2,1,0:T(8,128)(2,1)S(1)} %get-tuple-element.32.refs_8_), channel_id=1, source_target_pairs={{0,8},{4,12},{8,0},{12,4},{16,24},{20,28},{24,16},{28,20},{1,9},{5... | collective-permute-start | bytes 1572872 | tf_op jit(solution)/shard_map/ppermute | solution.py:148
  119.3 13.3 %collective-permute-start.3 = (bf16[2,32,4096]{2,1,0:T(8,128)(2,1)S(1)}, bf16[2,32,4096]{2,1,0:T(8,128)(2,1)S(1)}, u32[]{:S(2)}, u32[]{:S(2)}) collective-permute-start(bf16[2,32,4096]{2,1,0:T(8,128)(2,1)S(1)} %get-tuple-element.34), channel_id=1, source_target_pairs={{0,16},{4,20},{8,24},{12,28},{16,0},{20,4},{24,8},{28,12},{1,17},{... | collective-permute-start | bytes 1572872 | tf_op jit(solution)/shard_map/ppermute | solution.py:148
  120.9 16.7 %collective-permute-start.14 = (bf16[32,8192]{1,0:T(8,128)(2,1)S(1)}, bf16[32,8192]{1,0:T(8,128)(2,1)S(1)}, u32[]{:S(2)}, u32[]{:S(2)}) collective-permute-start(bf16[32,8192]{1,0:T(8,128)(2,1)S(1)} %collective-permute-done.10.refs_5_), channel_id=1, source_target_pairs={{1,2},{2,3},{5,6},{6,7},{9,10},{10,11},{13,14},{14,15},{17,18},{18... | collective-permute-start | bytes 1572872 | tf_op jit(solution)/shard_map/ppermute | solution.py:218
  131.3 21.5 %collective-permute-start.13 = (bf16[32,8192]{1,0:T(8,128)(2,1)S(1)}, bf16[32,8192]{1,0:T(8,128)(2,1)S(1)}, u32[]{:S(2)}, u32[]{:S(2)}) collective-permute-start(bf16[32,8192]{1,0:T(8,128)(2,1)S(1)} %collective-permute-done.12), channel_id=1, source_target_pairs={{1,0},{5,4},{9,8},{13,12},{17,16},{21,20},{25,24},{29,28}} | collective-permute-start | bytes 1572872 | tf_op jit(solution)/shard_map/ppermute | solution.py:219
  133.4 0.8 copy-start.2
  134.2 0.8 copy-start.3
  135.0 6.4 %collective-permute-start.8 = (bf16[1,32,4096]{2,1,0:T(8,128)(2,1)S(1)}, bf16[1,32,4096]{2,1,0:T(8,128)(2,1)S(1)}, u32[]{:S(2)}, u32[]{:S(2)}) collective-permute-start(bf16[1,32,4096]{2,1,0:T(8,128)(2,1)S(1)} %get-tuple-element.44.refs_4_), channel_id=1, source_target_pairs={{0,16},{4,20},{8,24},{12,28},{16,0},{20,4},{24,8},{28,12},{1,17},{... | collective-permute-start | bytes 786440 | tf_op jit(solution)/shard_map/ppermute | solution.py:148
  136.7 6.5 %collective-permute-start.9 = (bf16[1,32,4096]{2,1,0:T(8,128)(2,1)S(1)}, bf16[1,32,4096]{2,1,0:T(8,128)(2,1)}, u32[]{:S(2)}, u32[]{:S(2)}) collective-permute-start(bf16[1,32,4096]{2,1,0:T(8,128)(2,1)S(1)} %get-tuple-element.46), channel_id=1, source_target_pairs={{0,8},{4,12},{8,0},{12,4},{16,24},{20,28},{24,16},{28,20},{1,9},{5... | collective-permute-start | bytes 786440 | tf_op jit(solution)/shard_map/ppermute | solution.py:148
  137.5 17.1 %collective-permute-start.15 = (bf16[32,8192]{1,0:T(8,128)(2,1)S(1)}, bf16[32,8192]{1,0:T(8,128)(2,1)}, u32[]{:S(2)}, u32[]{:S(2)}) collective-permute-start(bf16[32,8192]{1,0:T(8,128)(2,1)S(1)} %collective-permute-done.14), channel_id=1, source_target_pairs={{2,3},{6,7},{10,11},{14,15},{18,19},{22,23},{26,27},{30,31}} | collective-permute-start | bytes 1572872 | tf_op jit(solution)/shard_map/ppermute | solution.py:218
  141.5 1.7 copy-start.8
  149.0 16.6 %collective-permute-start.16 = (bf16[32,8192]{1,0:T(8,128)(2,1)S(1)}, bf16[32,8192]{1,0:T(8,128)(2,1)S(1)}, u32[]{:S(2)}, u32[]{:S(2)}) collective-permute-start(bf16[32,8192]{1,0:T(8,128)(2,1)S(1)} %get-tuple-element.55), channel_id=1, source_target_pairs={{0,1},{1,2},{2,3},{3,0},{4,5},{5,6},{6,7},{7,4},{8,9},{9,10},{10,1... | collective-permute-start | bytes 1572872 | tf_op jit(solution)/shard_map/ppermute | solution.py:212
  151.7 21.3 %collective-permute-start.17 = (bf16[32,8192]{1,0:T(8,128)(2,1)S(1)}, bf16[32,8192]{1,0:T(8,128)(2,1)S(1)}, u32[]{:S(2)}, u32[]{:S(2)}) collective-permute-start(bf16[32,8192]{1,0:T(8,128)(2,1)S(1)} %get-tuple-element.55), channel_id=1, source_target_pairs={{1,0},{2,1},{3,2},{0,3},{5,4},{6,5},{7,6},{4,7},{9,8},{10,9},{11,1... | collective-permute-start | bytes 1572872 | tf_op jit(solution)/shard_map/ppermute | solution.py:213
  165.6 9.5 %collective-permute-start.18 = (bf16[32,8192]{1,0:T(8,128)(2,1)S(1)}, bf16[32,8192]{1,0:T(8,128)(2,1)S(1)}, u32[]{:S(2)}, u32[]{:S(2)}) collective-permute-start(bf16[32,8192]{1,0:T(8,128)(2,1)S(1)} %collective-permute-done.16), channel_id=1, source_target_pairs={{1,2},{2,3},{5,6},{6,7},{9,10},{10,11},{13,14},{14,15},{17,18},{18... | collective-permute-start | bytes 1572872 | tf_op jit(solution)/shard_map/ppermute | solution.py:214
  172.9 15.7 %collective-permute-start.19 = (bf16[32,8192]{1,0:T(8,128)(2,1)S(1)}, bf16[32,8192]{1,0:T(8,128)(2,1)S(1)}, u32[]{:S(2)}, u32[]{:S(2)}) collective-permute-start(bf16[32,8192]{1,0:T(8,128)(2,1)S(1)} %collective-permute-done.17), channel_id=1, source_target_pairs={{1,0},{2,1},{5,4},{6,5},{9,8},{10,9},{13,12},{14,13},{17,16},{18,1... | collective-permute-start | bytes 1572872 | tf_op jit(solution)/shard_map/ppermute | solution.py:215

commit v2 on v1

v2 whole, which is shorter than its diff:
```python
import functools
import jax
import jax.numpy as jnp
from jax import lax
from jax.experimental import pallas as pl
from jax.experimental.pallas import tpu as pltpu
from jax.sharding import PartitionSpec as P


beta_one = 0.9
beta_two = 0.95
learning_rate = 0.05
decay_rate = 0.1
epsilon = 1e-08
step_count = 4
LANES = 128
SUBLANES = 8
PARTS = (3, 1)
half = jnp.bfloat16
full = jnp.float32
ANY = pl.BlockSpec(memory_space=pl.ANY)
GRANT = pltpu.CompilerParams(vmem_limit_bytes=16 << 20)


def adamw(moment_one, moment_two, weights, gradient):
    new_one = beta_one * moment_one + (1.0 - beta_one) * gradient
    new_two = beta_two * moment_two + (1.0 - beta_two) * gradient * gradient
    unbiased_one = new_one * (1.0 / (1.0 - beta_one**step_count))
    unbiased_two = new_two * (1.0 / (1.0 - beta_two**step_count))
    updated = weights - learning_rate * (
        unbiased_one / (jnp.sqrt(unbiased_two) + epsilon) + decay_rate * weights
    )
    return (new_one, new_two, updated)


def owners(blocks, mapping, span):
    device = jnp.arange(mapping.shape[1], dtype=jnp.int32) // span
    found = blocks[:, :, None] == mapping[:, None, :]
    return jnp.sum(jnp.where(found, device[None, None, :], 0), axis=2)


def in_hbm(array):
    return pltpu.with_memory_space_constraint(array, pltpu.HBM)


def block(shape, where, start):
    width = shape[-1]
    if start % width == 0:
        return pl.BlockSpec(shape, lambda *at: (*where(*at), start // width))
    return pl.BlockSpec(
        tuple(pl.Element(size) for size in shape),
        lambda *at: (*(index * size for index, size in zip(where(*at), shape)), start),
    )


def cost(nbytes, flops=0):
    return pl.CostEstimate(flops=flops, bytes_accessed=nbytes, transcendentals=0)


def pack_kernel(by_shard, shards, dest, here, *refs):
    arrays, row_of = refs[:3], refs[-1]
    bands, depth, _ = arrays[0].shape
    span, sub = bands * SUBLANES, depth // SUBLANES
    outs = refs[3:-1]
    per_out = span // len(outs)

    @pl.when(pl.program_id(0) == 0)
    def _():
        for row in range(span):
            to = dest[row]
            if by_shard:
                to = lax.rem(lax.rem(to, shards) - here[0] + shards, shards) * per_out + lax.div(to, shards)
            row_of[to] = row

    for o, out in enumerate(outs):
        for slot in range(per_out):
            row = row_of[o * per_out + slot]
            band, first = lax.div(row, SUBLANES), lax.rem(row, SUBLANES)
            for k, array in enumerate(arrays):
                out[slot, k] = array[band, pl.ds(first, sub, stride=SUBLANES), :].astype(half)


def by_tile(array):
    span, width = array.shape
    tiled = array.reshape(span // SUBLANES, SUBLANES, width // LANES, LANES).transpose(0, 2, 1, 3)
    return tiled.reshape(span // SUBLANES, width // LANES * SUBLANES, LANES)


def pack(dest, here, arrays, start, width, shards, by_shard):
    span = arrays[0].shape[0]
    bands, tiles = span // SUBLANES, width // LANES
    steps = max(1, min(tiles // 16, 2))
    sub = tiles // steps
    count = shards if by_shard else 1
    deep = pl.BlockSpec((bands, sub * SUBLANES, LANES), lambda i, s, h: (0, start // (sub * LANES) + i, 0))
    shape = (span // count, 3, tiles, LANES)
    return pl.pallas_call(
        functools.partial(pack_kernel, by_shard, shards),
        out_shape=[jax.ShapeDtypeStruct(shape, half)] * count,
        grid_spec=pltpu.PrefetchScalarGridSpec(
            num_scalar_prefetch=2,
            grid=(steps,),
            in_specs=[deep] * 3,
            out_specs=[pl.BlockSpec((span // count, 3, sub, LANES), lambda i, s, h: (0, 0, i, 0))] * count,
            scratch_shapes=[pltpu.SMEM((span,), jnp.int32)],
        ),
        cost_estimate=cost(18 * span * width),
        compiler_params=GRANT,
    )(dest, here, *(in_hbm(by_tile(array)) for array in arrays))


def send_kernel(bits, grads, *refs):
    refs[-1][...] = grads[...]


def first_send(bits, grads, start, width):
    groups, span, _ = grads.shape
    return pl.pallas_call(
        send_kernel,
        out_shape=jax.ShapeDtypeStruct((groups // 2, span, width), half),
        grid_spec=pltpu.PrefetchScalarGridSpec(
            num_scalar_prefetch=1,
            grid=(groups // 2,),
            in_specs=[block((1, span, width), lambda i, b: (2 * i + 1 - b[0], 0), start)],
            out_specs=pl.BlockSpec((1, span, width), lambda i, b: (i, 0, 0)),
        ),
        cost_estimate=cost(2 * groups * span * width),
        compiler_params=GRANT,
    )(bits, in_hbm(grads))


def halve_kernel(bits, *refs):
    outs = refs[-4:]
    for k in range(4):
        total = refs[2 * k][...].astype(full) + refs[2 * k + 1][...].astype(full)
        outs[k][...] = total.astype(outs[k].dtype)


def halve(bits, parts, cut, span, last):
    specs, operands = [], []
    for kept, group, kept_col, came, came_col, left, bit in parts:
        place = left[::-1].index(bit)
        for keep in (False, True):

            def combo(i, b, place=place, bit=bit, keep=keep):
                value = b[bit] if keep else 1 - b[bit]
                return ((i >> place) << (place + 1)) | (value << place) | (i & ((1 << place) - 1))

            specs += [
                block((1, rows_of(span), cut), lambda i, r, b, combo=combo, group=group: (group(combo(i, b), b), r), kept_col),
                pl.BlockSpec((1, rows_of(span), cut), lambda i, r, b, combo=combo, col=came_col: (combo(i, b), r, col)),
            ]
            operands += [in_hbm(kept) if kept.ndim == 3 and kept.shape[-1] > cut else kept, came]
    combos = 1 << (len(parts[0][5]) - 1)
    out = pl.BlockSpec((1, rows_of(span), cut), lambda i, r, b: (i, r, 0))
    shape = (combos, span, cut)
    return pl.pallas_call(
        halve_kernel,
        out_shape=[jax.ShapeDtypeStruct(shape, half), jax.ShapeDtypeStruct(shape, full if last else half)] * 2,
        grid_spec=pltpu.PrefetchScalarGridSpec(
            num_scalar_prefetch=1,
            grid=(combos, span // rows_of(span)),
            in_specs=specs,
            out_specs=[out] * 4,
        ),
        cost_estimate=cost(24 * combos * span * cut),
        compiler_params=GRANT,
    )(bits, *operands)


def rows_of(span):
    return span // 2


def swap(part, bit):
    groups = lax.axis_size("dp")
    return lax.ppermute(part, "dp", [(i, i ^ (1 << bit)) for i in range(groups)])


def update_kernel(whole_step, source, here, *refs):
    rows_in, (keep_a, got_a, keep_b, got_b), states = refs[:SUBLANES], refs[SUBLANES : SUBLANES + 4], refs[-1]
    tiles = keep_a.shape[2] // LANES
    sub = 2 * tiles
    for row, row_in in enumerate(rows_in):
        came = row_in[0].astype(full)
        for k in range(3):
            states[k, pl.ds(row, sub, stride=SUBLANES), :] = came[k * sub : (k + 1) * sub]
    for kept, came, first in ((keep_a, got_a, 0), (keep_b, got_b, tiles)):
        for t in range(tiles):
            cols = slice(t * LANES, (t + 1) * LANES)
            out_cols = slice((first + t) * LANES, (first + t + 1) * LANES)
            rows = slice((first + t) * SUBLANES, (first + t + 1) * SUBLANES)
            gradient = kept[0, :, cols] + came[0, :, cols].astype(full)
            values = adamw(states[0, rows], states[1, rows], states[2, rows], gradient)
            if whole_step:
                for ref, value in zip(refs[-5:-1], values + values[2:]):
                    ref[:, out_cols] = value.astype(ref.dtype)
            else:
                refs[-2][:, out_cols] = values[2].astype(half)


def update(source, here, incoming, terms, carried, chunk, start, span, block_len, shards, by_shard, whole_step):
    sub = incoming.shape[1] // 3
    width = sub * LANES
    piece = pl.BlockSpec((1, SUBLANES, width // 2), lambda i, s, h: (0, i, 0))
    tile_rows = span // SUBLANES
    spread = {}

    def row_at(row):
        def index(i, s, h):
            at = s[i * SUBLANES + row]
            if by_shard:
                at = lax.div(at, shards) * shards + lax.rem(h[0] - lax.rem(at, shards) + shards, shards)
            return (at, 0, 0)

        return index

    if whole_step:
        wide = block((SUBLANES, width), lambda i, s, h: (i,), start)
        out_specs = [wide] * 3 + [block((SUBLANES, width), lambda i, s, h: (h[0] * tile_rows + i,), start)]
        outs = [jax.ShapeDtypeStruct((span, block_len), full)] * 3
        outs += [jax.ShapeDtypeStruct((shards * span, block_len), half)]
        if carried:
            spread = {6 + SUBLANES + o: o for o in range(4)}
    else:
        out_specs = [pl.BlockSpec((SUBLANES, width), lambda i, s, h: (i, 0))]
        outs = [jax.ShapeDtypeStruct((span, width), half)]
    call = pl.pallas_call(
        functools.partial(update_kernel, whole_step),
        out_shape=outs,
        grid_spec=pltpu.PrefetchScalarGridSpec(
            num_scalar_prefetch=2,
            grid=(tile_rows,),
            in_specs=[pl.BlockSpec((1, 3 * sub, LANES), row_at(row)) for row in range(SUBLANES)]
            + [piece] * 4
            + [ANY] * len(carried),
            out_specs=out_specs,
            scratch_shapes=[pltpu.VMEM((3, sub * SUBLANES, LANES), full)],
        ),
        input_output_aliases=spread,
        cost_estimate=cost(26 * span * width, 20 * span * width),
        compiler_params=GRANT,
    )
    held = in_hbm if chunk == 0 else lambda array: array
    return call(source, here, *[held(incoming)] * SUBLANES, *map(held, terms), *carried)


def exchange(outgoing):
    devices, _, tiles, _ = outgoing.shape
    came = lax.all_to_all(outgoing.reshape(devices, 3 * tiles, LANES), ("dp", "shard"), split_axis=0, concat_axis=0, tiled=True)
    return came


def travel(outgoing):
    n = lax.axis_size("shard")
    came = [outgoing[0]]
    for far in range(1, n):
        came.append(lax.ppermute(outgoing[far], "shard", [(i, (i + far) % n) for i in range(n)]))
    return came


def spread(came):
    groups, _, tiles, _ = came[0].shape
    stacked = jnp.stack(came, axis=1).reshape(groups, len(came) * 3 * tiles, LANES)
    came = lax.all_to_all(stacked, "dp", split_axis=0, concat_axis=0, tiled=True)
    return came.reshape(-1, 3 * tiles, LANES)


def gather_steps(block, direct):
    n = lax.axis_size("shard")

    def rotate(far):
        return lax.ppermute(block, "shard", [(i, (i + far) % n) for i in range(n)])

    if direct:
        return {far: (rotate(far),) * 2 for far in range(1, n)}
    if n == 4:
        near, back = rotate(1), rotate(3)
        over = lax.ppermute(near, "shard", [(i, i + 1) for i in range(1, n - 1)])
        under = lax.ppermute(back, "shard", [(i + 1, i) for i in range(n - 2)])
        return {1: (near, near), 3: (back, back), 2: (over, under)}
    up, down = {0: block}, {0: block}
    for step in range(1, n):
        up[step] = lax.ppermute(up[step - 1], "shard", [(i, i + 1) for i in range(step - 1, n - 1)])
        down[step] = lax.ppermute(down[step - 1], "shard", [(i + 1, i) for i in range(n - step)])
    return {far: (up[far], down[n - far]) for far in range(1, n)}


def place(whole, came, column):
    n = lax.axis_size("shard")
    here = lax.axis_index("shard")
    for far, (below, above) in came.items():
        value = below if below is above else jnp.where(here >= far, below, above)
        whole = lax.dynamic_update_slice(whole, value, ((here + n - far) % n * value.shape[0], column))
    return whole


def local(grad_parts, first_moment, second_moment, master, old_map, new_map):
    groups = lax.axis_size("dp")
    shards = lax.axis_size("shard")
    here = lax.axis_index("shard")
    replica = lax.axis_index("dp")
    mine = replica * shards + here
    span, block_len = first_moment.shape
    unit = block_len // sum(PARTS)
    parts_of = PARTS if unit % (2 * SUBLANES * LANES) == 0 else (1,)
    widths = [p * (block_len // sum(parts_of)) for p in parts_of]
    starts = [sum(widths[:c]) for c in range(len(widths))]
    chunks = len(widths)
    grads = grad_parts[0]
    maps = jnp.stack([old_map, new_map])
    dest, source = owners(lax.dynamic_slice_in_dim(maps, mine * span, span, 1), maps[::-1], span)
    at = here.reshape(1).astype(jnp.int32)
    steps = groups.bit_length() - 1
    bits = ((replica >> jnp.arange(steps, dtype=jnp.int32)) & 1).astype(jnp.int32)
    left = list(range(steps))[::-1][:-1]
    orders = (left[::-1], left)
    states = (first_moment, second_moment, master)

    def first_parts(c, came):
        return [
            (grads, lambda j, b: 2 * j + b[0], starts[c] + h * (widths[c] // 2), came, h, left, orders[h][0])
            for h in range(2)
        ]

    def next_parts(c, s, came):
        return [
            (sums[c][2 * h + 1], lambda j, b: j, 0, came[h], 0, [b for b in left if b not in orders[h][:s]], orders[h][s])
            for h in range(2)
        ]

    def swaps(c, s):
        return [swap(sums[c][2 * h], orders[h][s]) for h in range(2)]

    def summed(c):
        cut = widths[c] // 2
        came = swap(first_send(bits, grads, starts[c], widths[c]), 0)
        sums[c] = halve(bits, first_parts(c, came), cut, span, len(left) == 1)
        for s in range(1, len(left)):
            sums[c] = halve(bits, next_parts(c, s, swaps(c, s - 1)), cut, span, s == len(left) - 1)
        came = swaps(c, len(left) - 1)
        return [sums[c][1], came[0], sums[c][3], came[1]]

    sums, carried, gathered = {}, [], []
    for c in range(chunks):
        split = c > 0
        outgoing = pack(dest, at, states, starts[c], widths[c], shards, split)
        if split:
            incoming = spread(travel(outgoing))
        else:
            incoming = exchange(outgoing[0])
        given = (source, at, incoming, summed(c))
        sizes = (c, starts[c], span, block_len, shards, split)
        (weights,) = update(*given, [], *sizes, False)
        gathered.append(gather_steps(weights, False))
        carried = update(*given, carried, *sizes, True)
    one, two, new, whole = carried
    for c in range(chunks):
        whole = place(whole, gathered[c], starts[c])
    return (one, two, new, whole)


def solution(mesh):
    placed = (
        P("dp", None, "shard", None),
        P(("dp", "shard"), None),
        P(("dp", "shard"), None),
        P(("dp", "shard"), None),
        P(),
        P(),
    )
    return jax.shard_map(
        local,
        mesh=mesh,
        in_specs=placed,
        out_specs=(
            P(("dp", "shard"), None),
            P(("dp", "shard"), None),
            P(("dp", "shard"), None),
            P("dp", None),
        ),
        check_vma=False,
    )
```

time: 191 us -> 184 us (0.963)
  waiting for transfers between devices: 99.6 us -> 89.3 us
  Pallas kernels: 35.5 us -> 39.3 us
  starting transfers between devices: 38.4 us -> 41.6 us
    all_to_all x2, waiting for transfers between devices: 18.3 us -> 0.01 us  [the longest x1 0.01 us: exchange(): lax.all_to_all(outgoing.reshape(devices, 3 * tiles, LANES), ('dp', 'shard...]
    unnamed x22 -> x4, local copies, waits for them, and re-layouts: 8.02 us -> 1.8 us
    ppermute x1 -> x2, waiting for transfers between devices: 13.6 us -> 18.3 us  [gather_steps(): under = lax.ppermute(back, 'shard', [(i + 1, i) for i in range(n - 2)])]
    pallas_call x4 -> x6, Pallas kernels: 19.6 us -> 24.3 us  [the longest x4 17.5 us: update(): call(source, here, *[held(incoming)] * SUBLANES, *map(held, terms), *carr...]
    dynamic_update_slice x2 -> x4, local copies, waits for them, and re-layouts: 1.67 us -> 5.57 us  [place(): lax.dynamic_update_slice(whole, value, ((here + n - far) % n * value.shap...]
    ppermute x8 -> x7, waiting for transfers between devices: 34.8 us -> 37.3 us  [the longest x4 20.2 us: rotate(): return lax.ppermute(block, 'shard', [(i, (i + far) % n) for i in range(n)])]
    ppermute x8 -> x7, starting transfers between devices: 14.4 us -> 15.3 us  [the longest x4 8.43 us: rotate(): return lax.ppermute(block, 'shard', [(i, (i + far) % n) for i in range(n)])]
  transfers between devices with their start and end apart: 22 -> 23, of which waited for: 12 -> 10; matrix products, arithmetic and copies ran while one was open for 2% -> 4% of each run, Pallas kernels for 16% -> 19%
where the time goes in v2:
time: 184 us; the launch traced here: 183 us
  waiting for transfers between devices  89.3 us (49%)
  starting transfers between devices  41.6 us (23%)
  Pallas kernels  39.3 us (21%)
  local copies, waits for them, and re-layouts  8.52 us (5%)
  other arithmetic  3.61 us (2%)
    ppermute x10, waiting for transfers between devices, swap(): return lax.ppermute(part, 'dp', [(i, i ^ 1 << bit) for i in range(groups)])  33.7 us
    ppermute x4, waiting for transfers between devices, rotate(): return lax.ppermute(block, 'shard', [(i, (i + far) % n) for i in range(n)])  20.2 us
    ppermute x2, waiting for transfers between devices, gather_steps(): under = lax.ppermute(back, 'shard', [(i + 1, i) for i in range(n - 2)])  18.3 us
    pallas_call x4, Pallas kernels, update(): call(source, here, *[held(incoming)] * SUBLANES, *map(held, terms), *carr...  17.5 us
    ppermute x3, waiting for transfers between devices, travel(): lax.ppermute(outgoing[far], 'shard', [(i, (i + far) % n) for i in range(n)])  17.1 us
    ppermute x10, starting transfers between devices, swap(): return lax.ppermute(part, 'dp', [(i, i ^ 1 << bit) for i in range(groups)])  11.4 us
    pallas_call x4, Pallas kernels, halve(): pl.pallas_call(halve_kernel, out_shape=[jax.ShapeDtypeStruct(shape, half)...  9.17 us
    ppermute x4, starting transfers between devices, rotate(): return lax.ppermute(block, 'shard', [(i, (i + far) % n) for i in range(n)])  8.43 us
  transfers between devices with their start and end apart: 23, of which 10 were waited for; matrix products, arithmetic and copies ran while one was open for 4% of the time, Pallas kernels for 19%

profile of v2, /device:TPU:0, one launch (start us, length us, event | category | flops | bytes accessed | tf_op | source)
XLA Modules:
  0.0 183.3 jit_solution(4823319338117273485)
XLA Ops:
  0.7 0.7 pad_add_fusion
  1.4 0.8 fusion.3
  2.1 0.2 rev.3
  2.3 0.2 select_reduce_fusion
  2.5 4.5 %shard_map.97 = bf16[32,3,96,128]{3,2,1,0:T(8,128)(2,1)} custom-call(s32[32]{0:T(128)S(1)} %get-tuple-element.60.dest, s32[1]{0:T(128)} %bitcast.3.here, f32[4,1024,128]{2,1,0:T(8,128)} %bitcast.57, f32[4,1024,128]{2,1,0:T(8,128)} %bitcast.59, f32[4,1024,128]{2,1,0:T(8,128)} %bitcast.61), custom_call_target="tpu_custom_call" | custom-call | bytes 7077888 | tf_op jit(solution)/shard_map/pallas_call | solution.py:97
  7.1 7.4 %all-to-all-start.1 = ((bf16[32,288,128]{2,1,0:T(8,128)(2,1)}), bf16[32,288,128]{2,1,0:T(8,128)(2,1)}, u32[]{:S(2)}, u32[]{:S(2)}) async-start(bf16[32,288,128]{2,1,0:T(8,128)(2,1)} %bitcast.27), calls=%async_computation.1 | async-start | bytes 4718592 | tf_op jit(solution)/shard_map/all_to_all | solution.py:250
  14.5 3.2 %shard_map.98 = bf16[4,32,12288]{2,1,0:T(8,128)(2,1)S(1)} custom-call(s32[3]{0:T(128)S(1)} %shift-right-arithmetic_and_fusion.bits, bf16[8,32,16384]{2,1,0:T(8,128)(2,1)} %bitcast.47), custom_call_target="tpu_custom_call" | custom-call | bytes 6291456 | tf_op jit(solution)/shard_map/pallas_call | solution.py:118
  17.8 0.3 collective-permute-start.8
  18.0 5.5 %collective-permute-done.8.refs_1_.refs_3_.refs_5_.refs_7_ = bf16[4,32,12288]{2,1,0:T(8,128)(2,1)S(1)} collective-permute-done((bf16[4,32,12288]{2,1,0:T(8,128)(2,1)S(1)}, bf16[4,32,12288]{2,1,0:T(8,128)(2,1)S(1)}, u32[]{:S(2)}, u32[]{:S(2)}) %collective-permute-start.8) | collective-permute-done | bytes 3145760 | tf_op jit(solution)/shard_map/ppermute | solution.py:177
  23.5 3.9 %shard_map.99 = (bf16[2,32,6144]{2,1,0:T(8,128)(2,1)S(1)}, bf16[2,32,6144]{2,1,0:T(8,128)(2,1)S(1)}, bf16[2,32,6144]{2,1,0:T(8,128)(2,1)S(1)}, bf16[2,32,6144]{2,1,0:T(8,128)(2,1)S(1)}) custom-call(s32[3]{0:T(128)S(1)} %shift-right-arithmetic_and_fusion.bits, bf16[8,32,16384]{2,1,0:T(8,128)(2,1)} %bitcast.48, ...), custom_call_target="tpu_custom_call" | custom-call | bytes 9437184 | tf_op jit(solution)/shard_map/pallas_call | solution.py:157
  27.4 1.8 collective-permute-start.10
  29.2 1.5 collective-permute-start.9
  30.6 2.6 %shard_map.94 = bf16[4,32,4096]{2,1,0:T(8,128)(2,1)S(1)} custom-call(s32[3]{0:T(128)S(1)} %shift-right-arithmetic_and_fusion.bits, bf16[8,32,16384]{2,1,0:T(8,128)(2,1)} %bitcast.52), custom_call_target="tpu_custom_call" | custom-call | bytes 2097152 | tf_op jit(solution)/shard_map/pallas_call | solution.py:118
  33.3 0.1 collective-permute-start.3
  33.3 2.2 %shard_map.93 = (bf16[8,3,32,128]{3,2,1,0:T(8,128)(2,1)S(1)}, bf16[8,3,32,128]{3,2,1,0:T(8,128)(2,1)S(1)}, bf16[8,3,32,128]{3,2,1,0:T(8,128)(2,1)S(1)}, bf16[8,3,32,128]{3,2,1,0:T(8,128)(2,1)S(1)}) custom-call(s32[32]{0:T(128)S(1)} %get-tuple-element.60.dest, s32[1]{0:T(128)} %bitcast.3.here, f32[4,1024,128]{2,1,0:T(8,128)} %bitcast.58, ...), custom_call_target="tpu_custom_call" | custom-call | bytes 2359296 | tf_op jit(solution)/shard_map/pallas_call | solution.py:97
  35.6 1.5 collective-permute-start
  37.1 2.5 %collective-permute-start.1 = (bf16[8,3,32,128]{3,2,1,0:T(8,128)(2,1)S(1)}, bf16[8,3,32,128]{3,2,1,0:T(8,128)(2,1)S(1)}, u32[]{:S(2)}, u32[]{:S(2)}) collective-permute-start(bf16[8,3,32,128]{3,2,1,0:T(8,128)(2,1)S(1)} %get-tuple-element.34), channel_id=1, source_target_pairs={{0,2},{1,3},{2,0},{3,1},{4,6},{5,7},{6,4},{7,5},{8,10},{9,11},{10,... | collective-permute-start | bytes 589832 | tf_op jit(solution)/shard_map/ppermute | solution.py:258
  39.6 17.6 %collective-permute-done.10.refs_5_.refs_7_ = bf16[2,32,6144]{2,1,0:T(8,128)(2,1)S(1)} collective-permute-done((bf16[2,32,6144]{2,1,0:T(8,128)(2,1)S(1)}, bf16[2,32,6144]{2,1,0:T(8,128)(2,1)S(1)}, u32[]{:S(2)}, u32[]{:S(2)}) %collective-permute-start.10) | collective-permute-done | bytes 786464 | tf_op jit(solution)/shard_map/ppermute | solution.py:177
  57.1 2.9 %collective-permute-start.2 = (bf16[8,3,32,128]{3,2,1,0:T(8,128)(2,1)S(1)}, bf16[8,3,32,128]{3,2,1,0:T(8,128)(2,1)S(1)}, u32[]{:S(2)}, u32[]{:S(2)}) collective-permute-start(bf16[8,3,32,128]{3,2,1,0:T(8,128)(2,1)S(1)} %get-tuple-element.35), channel_id=1, source_target_pairs={{0,3},{1,0},{2,1},{3,2},{4,7},{5,4},{6,5},{7,6},{8,11},{9,8},{10,9... | collective-permute-start | bytes 589832 | tf_op jit(solution)/shard_map/ppermute | solution.py:258
  60.0 0.0 collective-permute-done.9.refs_1_.refs_3_
  60.0 1.5 shard_map.100
  61.6 0.9 copy-done
  62.5 0.9 copy-done.1
  63.4 0.8 collective-permute-start.11
  64.2 0.0 collective-permute-done
  64.2 1.5 collective-permute-start.12
  65.6 17.1 %collective-permute-done.1 = bf16[8,3,32,128]{3,2,1,0:T(8,128)(2,1)S(1)} collective-permute-done((bf16[8,3,32,128]{3,2,1,0:T(8,128)(2,1)S(1)}, bf16[8,3,32,128]{3,2,1,0:T(8,128)(2,1)S(1)}, u32[]{:S(2)}, u32[]{:S(2)}) %collective-permute-start.1) | collective-permute-done | bytes 196640 | tf_op jit(solution)/shard_map/ppermute | solution.py:258
  82.8 0.1 pad_maximum_fusion
  82.9 1.0 copy.15
  83.8 0.0 all-to-all-done.1.refs_0_.refs_1_.refs_2_.refs_3_.refs_4_.refs_5_.refs_6_.refs_7_
  83.8 3.5 %all-to-all-start = ((bf16[8,384,128]{2,1,0:T(8,128)(2,1)}), bf16[8,384,128]{2,1,0:T(8,128)(2,1)S(1)}, u32[]{:S(2)}, u32[]{:S(2)}) async-start(bf16[8,384,128]{2,1,0:T(8,128)(2,1)} %bitcast.63), calls=%async_computation | async-start | bytes 1572864 | tf_op jit(solution)/shard_map/all_to_all | solution.py:265
  87.4 0.0 collective-permute-done.12.refs_11_
  87.4 6.2 %shard_map.103 = bf16[32,12288]{1,0:T(8,128)(2,1)} custom-call(s32[32]{0:T(128)S(1)} %get-tuple-element.61.source, s32[1]{0:T(128)} %bitcast.3.here, bf16[32,288,128]{2,1,0:T(8,128)(2,1)} %all-to-all-done.1.refs_0_.refs_1_.refs_2_.refs_3_.refs_4_.refs_5_.refs_6_.refs_7_, ...), custom_call_target="tpu_custom_call" | custom-call | flops 7864320 | bytes 10223616 | tf_op jit(solution)/shard_map/pallas_call | solution.py:245
  93.6 4.2 %collective-permute-start.13 = (bf16[32,12288]{1,0:T(8,128)(2,1)}, bf16[32,12288]{1,0:T(8,128)(2,1)}, u32[]{:S(2)}, u32[]{:S(2)}) collective-permute-start(bf16[32,12288]{1,0:T(8,128)(2,1)} %shard_map.103), channel_id=1, source_target_pairs={{0,1},{1,2},{2,3},{3,0},{4,5},{5,6},{6,7},{7,4},{8,9},{9,10},{10,1... | collective-permute-start | bytes 2359304 | tf_op jit(solution)/shard_map/ppermute | solution.py:273
  97.8 0.3 collective-permute-start.14
  98.1 0.0 collective-permute-done.3.refs_1_.refs_3_.refs_5_.refs_7_
  98.1 3.0 %shard_map.95 = (bf16[2,32,2048]{2,1,0:T(8,128)(2,1)S(1)}, bf16[2,32,2048]{2,1,0:T(8,128)(2,1)S(1)}, bf16[2,32,2048]{2,1,0:T(8,128)(2,1)S(1)}, bf16[2,32,2048]{2,1,0:T(8,128)(2,1)S(1)}) custom-call(s32[3]{0:T(128)S(1)} %shift-right-arithmetic_and_fusion.bits, bf16[8,32,16384]{2,1,0:T(8,128)(2,1)} %bitcast.53, ...), custom_call_target="tpu_custom_call" | custom-call | bytes 3145728 | tf_op jit(solution)/shard_map/pallas_call | solution.py:157
  101.1 2.0 %collective-permute-start.4 = (bf16[2,32,2048]{2,1,0:T(8,128)(2,1)S(1)}, bf16[2,32,2048]{2,1,0:T(8,128)(2,1)S(1)}, u32[]{:S(2)}, u32[]{:S(2)}) collective-permute-start(bf16[2,32,2048]{2,1,0:T(8,128)(2,1)S(1)} %get-tuple-element.37), channel_id=1, source_target_pairs={{0,8},{4,12},{8,0},{12,4},{16,24},{20,28},{24,16},{28,20},{1,9},{5... | collective-permute-start | bytes 786440 | tf_op jit(solution)/shard_map/ppermute | solution.py:177
  103.1 1.5 collective-permute-start.5
  104.6 4.9 %collective-permute-done.4.refs_1_.refs_3_ = bf16[2,32,2048]{2,1,0:T(8,128)(2,1)S(1)} collective-permute-done((bf16[2,32,2048]{2,1,0:T(8,128)(2,1)S(1)}, bf16[2,32,2048]{2,1,0:T(8,128)(2,1)S(1)}, u32[]{:S(2)}, u32[]{:S(2)}) %collective-permute-start.4) | collective-permute-done | bytes 262176 | tf_op jit(solution)/shard_map/ppermute | solution.py:177
  109.5 1.4 collective-permute-done.5.refs_5_.refs_7_
  110.9 0.7 shard_map.96
  111.6 1.6 collective-permute-start.6
  113.2 0.5 collective-permute-start.7
  113.7 2.9 %collective-permute-done.6.refs_9_ = bf16[1,32,2048]{2,1,0:T(8,128)(2,1)S(1)} collective-permute-done((bf16[1,32,2048]{2,1,0:T(8,128)(2,1)S(1)}, bf16[1,32,2048]{2,1,0:T(8,128)(2,1)S(1)}, u32[]{:S(2)}, u32[]{:S(2)}) %collective-permute-start.6) | collective-permute-done | bytes 131104 | tf_op jit(solution)/shard_map/ppermute | solution.py:177
  116.7 1.5 collective-permute-done.7.refs_11_
  118.1 1.6 shard_map.104
  119.7 1.5 collective-permute-start.17
  121.2 2.4 %collective-permute-start.18 = (bf16[32,4096]{1,0:T(8,128)(2,1)S(1)}, bf16[32,4096]{1,0:T(8,128)(2,1)S(1)}, u32[]{:S(2)}, u32[]{:S(2)}) collective-permute-start(bf16[32,4096]{1,0:T(8,128)(2,1)S(1)} %shard_map.104), channel_id=1, source_target_pairs={{0,3},{1,0},{2,1},{3,2},{4,7},{5,4},{6,5},{7,6},{8,11},{9,8},{10,9... | collective-permute-start | bytes 786440 | tf_op jit(solution)/shard_map/ppermute | solution.py:273
  123.6 15.6 %collective-permute-done.17 = bf16[32,4096]{1,0:T(8,128)(2,1)S(1)} collective-permute-done((bf16[32,4096]{1,0:T(8,128)(2,1)S(1)}, bf16[32,4096]{1,0:T(8,128)(2,1)S(1)}, u32[]{:S(2)}, u32[]{:S(2)}) %collective-permute-start.17) | collective-permute-done | bytes 262176 | tf_op jit(solution)/shard_map/ppermute | solution.py:273
  139.2 0.7 collective-permute-start.19
  139.9 4.6 %collective-permute-done.18 = bf16[32,4096]{1,0:T(8,128)(2,1)S(1)} collective-permute-done((bf16[32,4096]{1,0:T(8,128)(2,1)S(1)}, bf16[32,4096]{1,0:T(8,128)(2,1)S(1)}, u32[]{:S(2)}, u32[]{:S(2)}) %collective-permute-start.18) | collective-permute-done | bytes 262176 | tf_op jit(solution)/shard_map/ppermute | solution.py:273
  144.5 1.3 collective-permute-start.20
  145.8 7.0 %shard_map.101 = (f32[32,16384]{1,0:T(8,128)}, f32[32,16384]{1,0:T(8,128)}, f32[32,16384]{1,0:T(8,128)}, bf16[128,16384]{1,0:T(8,128)(2,1)}) custom-call(s32[32]{0:T(128)S(1)} %get-tuple-element.61.source, s32[1]{0:T(128)} %bitcast.3.here, bf16[32,288,128]{2,1,0:T(8,128)(2,1)} %all-to-all-done.1.refs_0_.refs_1_.refs_2_.refs_3_.refs_4_.refs_5_.refs_6_.refs_7_, ...), custom_call_target="tpu_custom_call" | custom-call | flops 7864320 | bytes 10223616 | tf_op jit(solution)/shard_map/pallas_call | solution.py:245
  152.8 2.8 %shard_map.102 = (f32[32,16384]{1,0:T(8,128)}, f32[32,16384]{1,0:T(8,128)}, f32[32,16384]{1,0:T(8,128)}, bf16[128,16384]{1,0:T(8,128)(2,1)}) custom-call(s32[32]{0:T(128)S(1)} %get-tuple-element.61.source, s32[1]{0:T(128)} %bitcast.3.here, ...), custom_call_target="tpu_custom_call", output_to_operand_aliasing={{0}: (14, {}), {1}: (15, {}), {2}: (16, {}), {3}: (17, {})} | custom-call | flops 2621440 | bytes 3407872 | tf_op jit(solution)/shard_map/pallas_call | solution.py:245
  155.6 0.7 collective-permute-start.15
  156.3 1.3 collective-permute-start.16
  157.6 2.1 %constant_dynamic-update-slice_fusion.1 = bf16[128,16384]{1,0:T(8,128)(2,1)} fusion(bf16[128,16384]{1,0:T(8,128)(2,1)} %get-tuple-element.59, bf16[32,12288]{1,0:T(8,128)(2,1)} %collective-permute-done.13, s32[]{:T(128)S(6)} %select_n.69), kind=kLoop, calls=%fused_computation.15 | loop fusion | bytes 1572868 | tf_op jit(solution)/shard_map/dynamic_update_slice | solution.py:294
  159.7 2.1 %constant_dynamic-update-slice_fusion = bf16[128,16384]{1,0:T(8,128)(2,1)} fusion(bf16[128,16384]{1,0:T(8,128)(2,1)} %constant_dynamic-update-slice_fusion.1, bf16[32,12288]{1,0:T(8,128)(2,1)} %collective-permute-done.14, s32[]{:T(128)S(6)} %select_n.71), kind=kLoop, calls=%fused_computation.14 | loop fusion | bytes 1572868 | tf_op jit(solution)/shard_map/dynamic_update_slice | solution.py:294
  161.7 18.3 %collective-permute-done.16 = bf16[32,12288]{1,0:T(8,128)(2,1)S(1)} collective-permute-done((bf16[32,12288]{1,0:T(8,128)(2,1)}, bf16[32,12288]{1,0:T(8,128)(2,1)S(1)}, u32[]{:S(2)}, u32[]{:S(2)}) %collective-permute-start.16) | collective-permute-done | bytes 786464 | tf_op jit(solution)/shard_map/ppermute | solution.py:280
  180.0 1.1 select_dynamic-update-slice_fusion
  181.1 0.7 constant_dynamic-update-slice_fusion.3
  181.8 0.7 constant_dynamic-update-slice_fusion.2
  182.5 0.8 select_dynamic-update-slice_fusion.1
  (13 shorter events, 0.0 us)
Async XLA Ops:
  7.1 76.8 %all-to-all-start.1 = ((bf16[32,288,128]{2,1,0:T(8,128)(2,1)}), bf16[32,288,128]{2,1,0:T(8,128)(2,1)}, u32[]{:S(2)}, u32[]{:S(2)}) async-start(bf16[32,288,128]{2,1,0:T(8,128)(2,1)} %bitcast.27), calls=%async_computation.1 | async-start | bytes 4718592 | tf_op jit(solution)/shard_map/all_to_all | solution.py:250
  17.8 5.7 %collective-permute-start.8 = (bf16[4,32,12288]{2,1,0:T(8,128)(2,1)S(1)}, bf16[4,32,12288]{2,1,0:T(8,128)(2,1)S(1)}, u32[]{:S(2)}, u32[]{:S(2)}) collective-permute-start(bf16[4,32,12288]{2,1,0:T(8,128)(2,1)S(1)} %shard_map.98), channel_id=1, source_target_pairs={{0,4},{4,0},{8,12},{12,8},{16,20},{20,16},{24,28},{28,24},{1,5},{5... | collective-permute-start | bytes 9437192 | tf_op jit(solution)/shard_map/ppermute | solution.py:177
  27.4 29.7 %collective-permute-start.10 = (bf16[2,32,6144]{2,1,0:T(8,128)(2,1)S(1)}, bf16[2,32,6144]{2,1,0:T(8,128)(2,1)S(1)}, u32[]{:S(2)}, u32[]{:S(2)}) collective-permute-start(bf16[2,32,6144]{2,1,0:T(8,128)(2,1)S(1)} %get-tuple-element.47), channel_id=1, source_target_pairs={{0,16},{4,20},{8,24},{12,28},{16,0},{20,4},{24,8},{28,12},{1,17},{... | collective-permute-start | bytes 2359304 | tf_op jit(solution)/shard_map/ppermute | solution.py:177
  29.2 30.9 %collective-permute-start.9 = (bf16[2,32,6144]{2,1,0:T(8,128)(2,1)S(1)}, bf16[2,32,6144]{2,1,0:T(8,128)(2,1)S(1)}, u32[]{:S(2)}, u32[]{:S(2)}) collective-permute-start(bf16[2,32,6144]{2,1,0:T(8,128)(2,1)S(1)} %get-tuple-element.45), channel_id=1, source_target_pairs={{0,8},{4,12},{8,0},{12,4},{16,24},{20,28},{24,16},{28,20},{1,9},{5... | collective-permute-start | bytes 2359304 | tf_op jit(solution)/shard_map/ppermute | solution.py:177
  33.3 64.9 %collective-permute-start.3 = (bf16[4,32,4096]{2,1,0:T(8,128)(2,1)S(1)}, bf16[4,32,4096]{2,1,0:T(8,128)(2,1)S(1)}, u32[]{:S(2)}, u32[]{:S(2)}) collective-permute-start(bf16[4,32,4096]{2,1,0:T(8,128)(2,1)S(1)} %shard_map.94), channel_id=1, source_target_pairs={{0,4},{4,0},{8,12},{12,8},{16,20},{20,16},{24,28},{28,24},{1,5},{5... | collective-permute-start | bytes 3145736 | tf_op jit(solution)/shard_map/ppermute | solution.py:177
  35.6 28.6 %collective-permute-start = (bf16[8,3,32,128]{3,2,1,0:T(8,128)(2,1)S(1)}, bf16[8,3,32,128]{3,2,1,0:T(8,128)(2,1)S(1)}, u32[]{:S(2)}, u32[]{:S(2)}) collective-permute-start(bf16[8,3,32,128]{3,2,1,0:T(8,128)(2,1)S(1)} %get-tuple-element.33), channel_id=1, source_target_pairs={{0,1},{1,2},{2,3},{3,0},{4,5},{5,6},{6,7},{7,4},{8,9},{9,10},{10,1... | collective-permute-start | bytes 589832 | tf_op jit(solution)/shard_map/ppermute | solution.py:258
  37.1 45.7 %collective-permute-start.1 = (bf16[8,3,32,128]{3,2,1,0:T(8,128)(2,1)S(1)}, bf16[8,3,32,128]{3,2,1,0:T(8,128)(2,1)S(1)}, u32[]{:S(2)}, u32[]{:S(2)}) collective-permute-start(bf16[8,3,32,128]{3,2,1,0:T(8,128)(2,1)S(1)} %get-tuple-element.34), channel_id=1, source_target_pairs={{0,2},{1,3},{2,0},{3,1},{4,6},{5,7},{6,4},{7,5},{8,10},{9,11},{10,... | collective-permute-start | bytes 589832 | tf_op jit(solution)/shard_map/ppermute | solution.py:258
  57.1 25.6 %collective-permute-start.2 = (bf16[8,3,32,128]{3,2,1,0:T(8,128)(2,1)S(1)}, bf16[8,3,32,128]{3,2,1,0:T(8,128)(2,1)S(1)}, u32[]{:S(2)}, u32[]{:S(2)}) collective-permute-start(bf16[8,3,32,128]{3,2,1,0:T(8,128)(2,1)S(1)} %get-tuple-element.35), channel_id=1, source_target_pairs={{0,3},{1,0},{2,1},{3,2},{4,7},{5,4},{6,5},{7,6},{8,11},{9,8},{10,9... | collective-permute-start | bytes 589832 | tf_op jit(solution)/shard_map/ppermute | solution.py:258
  61.6 0.9 copy-start
  62.5 0.9 copy-start.1
  63.4 24.0 %collective-permute-start.11 = (bf16[1,32,6144]{2,1,0:T(8,128)(2,1)}, bf16[1,32,6144]{2,1,0:T(8,128)(2,1)}, u32[]{:S(2)}, u32[]{:S(2)}) collective-permute-start(bf16[1,32,6144]{2,1,0:T(8,128)(2,1)} %get-tuple-element.49), channel_id=1, source_target_pairs={{0,16},{4,20},{8,24},{12,28},{16,0},{20,4},{24,8},{28,12},{1,17},{... | collective-permute-start | bytes 1179656 | tf_op jit(solution)/shard_map/ppermute | solution.py:177
  64.2 23.2 %collective-permute-start.12 = (bf16[1,32,6144]{2,1,0:T(8,128)(2,1)S(1)}, bf16[1,32,6144]{2,1,0:T(8,128)(2,1)}, u32[]{:S(2)}, u32[]{:S(2)}) collective-permute-start(bf16[1,32,6144]{2,1,0:T(8,128)(2,1)S(1)} %get-tuple-element.51), channel_id=1, source_target_pairs={{0,8},{4,12},{8,0},{12,4},{16,24},{20,28},{24,16},{28,20},{1,9},{5... | collective-permute-start | bytes 1179656 | tf_op jit(solution)/shard_map/ppermute | solution.py:177
  83.8 29.9 %all-to-all-start = ((bf16[8,384,128]{2,1,0:T(8,128)(2,1)}), bf16[8,384,128]{2,1,0:T(8,128)(2,1)S(1)}, u32[]{:S(2)}, u32[]{:S(2)}) async-start(bf16[8,384,128]{2,1,0:T(8,128)(2,1)} %bitcast.63), calls=%async_computation | async-start | bytes 1572864 | tf_op jit(solution)/shard_map/all_to_all | solution.py:265
  93.6 62.0 %collective-permute-start.13 = (bf16[32,12288]{1,0:T(8,128)(2,1)}, bf16[32,12288]{1,0:T(8,128)(2,1)}, u32[]{:S(2)}, u32[]{:S(2)}) collective-permute-start(bf16[32,12288]{1,0:T(8,128)(2,1)} %shard_map.103), channel_id=1, source_target_pairs={{0,1},{1,2},{2,3},{3,0},{4,5},{5,6},{6,7},{7,4},{8,9},{9,10},{10,1... | collective-permute-start | bytes 2359304 | tf_op jit(solution)/shard_map/ppermute | solution.py:273
  97.8 58.5 %collective-permute-start.14 = (bf16[32,12288]{1,0:T(8,128)(2,1)}, bf16[32,12288]{1,0:T(8,128)(2,1)}, u32[]{:S(2)}, u32[]{:S(2)}) collective-permute-start(bf16[32,12288]{1,0:T(8,128)(2,1)} %shard_map.103), channel_id=1, source_target_pairs={{0,3},{1,0},{2,1},{3,2},{4,7},{5,4},{6,5},{7,6},{8,11},{9,8},{10,9... | collective-permute-start | bytes 2359304 | tf_op jit(solution)/shard_map/ppermute | solution.py:273
  101.1 8.4 %collective-permute-start.4 = (bf16[2,32,2048]{2,1,0:T(8,128)(2,1)S(1)}, bf16[2,32,2048]{2,1,0:T(8,128)(2,1)S(1)}, u32[]{:S(2)}, u32[]{:S(2)}) collective-permute-start(bf16[2,32,2048]{2,1,0:T(8,128)(2,1)S(1)} %get-tuple-element.37), channel_id=1, source_target_pairs={{0,8},{4,12},{8,0},{12,4},{16,24},{20,28},{24,16},{28,20},{1,9},{5... | collective-permute-start | bytes 786440 | tf_op jit(solution)/shard_map/ppermute | solution.py:177
  103.1 7.8 %collective-permute-start.5 = (bf16[2,32,2048]{2,1,0:T(8,128)(2,1)S(1)}, bf16[2,32,2048]{2,1,0:T(8,128)(2,1)S(1)}, u32[]{:S(2)}, u32[]{:S(2)}) collective-permute-start(bf16[2,32,2048]{2,1,0:T(8,128)(2,1)S(1)} %get-tuple-element.39), channel_id=1, source_target_pairs={{0,16},{4,20},{8,24},{12,28},{16,0},{20,4},{24,8},{28,12},{1,17},{... | collective-permute-start | bytes 786440 | tf_op jit(solution)/shard_map/ppermute | solution.py:177
  111.6 5.0 %collective-permute-start.6 = (bf16[1,32,2048]{2,1,0:T(8,128)(2,1)S(1)}, bf16[1,32,2048]{2,1,0:T(8,128)(2,1)S(1)}, u32[]{:S(2)}, u32[]{:S(2)}) collective-permute-start(bf16[1,32,2048]{2,1,0:T(8,128)(2,1)S(1)} %get-tuple-element.41), channel_id=1, source_target_pairs={{0,16},{4,20},{8,24},{12,28},{16,0},{20,4},{24,8},{28,12},{1,17},{... | collective-permute-start | bytes 393224 | tf_op jit(solution)/shard_map/ppermute | solution.py:177
  113.2 5.0 %collective-permute-start.7 = (bf16[1,32,2048]{2,1,0:T(8,128)(2,1)S(1)}, bf16[1,32,2048]{2,1,0:T(8,128)(2,1)S(1)}, u32[]{:S(2)}, u32[]{:S(2)}) collective-permute-start(bf16[1,32,2048]{2,1,0:T(8,128)(2,1)S(1)} %get-tuple-element.43), channel_id=1, source_target_pairs={{0,8},{4,12},{8,0},{12,4},{16,24},{20,28},{24,16},{28,20},{1,9},{5... | collective-permute-start | bytes 393224 | tf_op jit(solution)/shard_map/ppermute | solution.py:177
  119.7 19.5 %collective-permute-start.17 = (bf16[32,4096]{1,0:T(8,128)(2,1)S(1)}, bf16[32,4096]{1,0:T(8,128)(2,1)S(1)}, u32[]{:S(2)}, u32[]{:S(2)}) collective-permute-start(bf16[32,4096]{1,0:T(8,128)(2,1)S(1)} %shard_map.104), channel_id=1, source_target_pairs={{0,1},{1,2},{2,3},{3,0},{4,5},{5,6},{6,7},{7,4},{8,9},{9,10},{10,1... | collective-permute-start | bytes 786440 | tf_op jit(solution)/shard_map/ppermute | solution.py:273
  121.2 23.3 %collective-permute-start.18 = (bf16[32,4096]{1,0:T(8,128)(2,1)S(1)}, bf16[32,4096]{1,0:T(8,128)(2,1)S(1)}, u32[]{:S(2)}, u32[]{:S(2)}) collective-permute-start(bf16[32,4096]{1,0:T(8,128)(2,1)S(1)} %shard_map.104), channel_id=1, source_target_pairs={{0,3},{1,0},{2,1},{3,2},{4,7},{5,4},{6,5},{7,6},{8,11},{9,8},{10,9... | collective-permute-start | bytes 786440 | tf_op jit(solution)/shard_map/ppermute | solution.py:273
  139.2 43.3 %collective-permute-start.19 = (bf16[32,4096]{1,0:T(8,128)(2,1)S(1)}, bf16[32,4096]{1,0:T(8,128)(2,1)S(1)}, u32[]{:S(2)}, u32[]{:S(2)}) collective-permute-start(bf16[32,4096]{1,0:T(8,128)(2,1)S(1)} %collective-permute-done.17), channel_id=1, source_target_pairs={{1,2},{2,3},{5,6},{6,7},{9,10},{10,11},{13,14},{14,15},{17,18},{18... | collective-permute-start | bytes 786440 | tf_op jit(solution)/shard_map/ppermute | solution.py:279
  144.5 38.0 %collective-permute-start.20 = (bf16[32,4096]{1,0:T(8,128)(2,1)S(1)}, bf16[32,4096]{1,0:T(8,128)(2,1)S(1)}, u32[]{:S(2)}, u32[]{:S(2)}) collective-permute-start(bf16[32,4096]{1,0:T(8,128)(2,1)S(1)} %collective-permute-done.18), channel_id=1, source_target_pairs={{1,0},{2,1},{5,4},{6,5},{9,8},{10,9},{13,12},{14,13},{17,16},{18,1... | collective-permute-start | bytes 786440 | tf_op jit(solution)/shard_map/ppermute | solution.py:280
  155.6 6.2 %collective-permute-start.15 = (bf16[32,12288]{1,0:T(8,128)(2,1)}, bf16[32,12288]{1,0:T(8,128)(2,1)S(1)}, u32[]{:S(2)}, u32[]{:S(2)}) collective-permute-start(bf16[32,12288]{1,0:T(8,128)(2,1)} %collective-permute-done.13), channel_id=1, source_target_pairs={{1,2},{2,3},{5,6},{6,7},{9,10},{10,11},{13,14},{14,15},{17,18},{18... | collective-permute-start | bytes 2359304 | tf_op jit(solution)/shard_map/ppermute | solution.py:279
  156.3 23.7 %collective-permute-start.16 = (bf16[32,12288]{1,0:T(8,128)(2,1)}, bf16[32,12288]{1,0:T(8,128)(2,1)S(1)}, u32[]{:S(2)}, u32[]{:S(2)}) collective-permute-start(bf16[32,12288]{1,0:T(8,128)(2,1)} %collective-permute-done.14), channel_id=1, source_target_pairs={{1,0},{2,1},{5,4},{6,5},{9,8},{10,9},{13,12},{14,13},{17,16},{18,1... | collective-permute-start | bytes 2359304 | tf_op jit(solution)/shard_map/ppermute | solution.py:280
